TPU v7x, 512 devices: a whole 4x4x16 slice. The times are simulated.
512 devices in a mesh: sky: 16 (over z), tile: 32 (over y, x, core).
Axes of the slice: x: 4, y: 4, z: 16, core: 2. Of those that a mesh axis runs over, the one named last changes fastest.
Arguments:
- science: float32 [16, 32, 2, 128, 512], P('sky', 'tile'), may hold values from -6 to 6
- inverse_variance: bfloat16 [16, 32, 2, 128, 512], P('sky', 'tile'), may hold values from 0.25 to 4
- template: bfloat16 [16, 32, 128, 512], P('sky', 'tile'), may hold values from -6 to 6
- filters: bfloat16 [8, 21], replicated, may hold values from -1.25 to 1.25
- kernel_index: int32 [20, 2], replicated, may hold values from 0 to 7
- spatial_coeff: float32 [16, 32, 2, 3, 20], P('sky', 'tile'), may hold values from -1.5 to 1.5
- visit_offset: int32 [16, 2], P('sky'), may hold values from 0 to 31
- block_count: int32 [16, 32, 2], P('sky', 'tile'), may hold values from 12 to 16, as said below
- block_owner: int32 [16, 32, 32], P('sky', 'tile'), may hold values from 0 to 31, as said below
- block_slot: int32 [16, 32, 32], P('sky', 'tile'), may hold values from 0 to 2
- coadd_sum: float32 [16, 32, 3, 4096], P('sky', 'tile'), may hold values from -18 to 18
- coadd_weight: float32 [16, 32, 3, 4096], P('sky', 'tile'), may hold values from 2 to 8
Outputs:
- difference: float32 [16, 32, 2, 128, 512], P('sky', 'tile')
- coadd: float32 [16, 32, 3, 4096], P('sky', 'tile')
Inputs may be any that keep to these rules, and one draw needn't show every extreme that they name: `visit_offset`: exposure tile i of a group lies in visit v on template tile (i + offset) mod 32. `block_count`: blocks 0 to count - 1 of a tile and visit enter the coadd. `block_owner`: among the 32 blocks of one device no owner appears more than 2 times; in each sky group one owner receives exactly 2 blocks from every device of the group, their first 2 blocks.
All inputs are finite; a program needn't handle non-finite values.
Results may differ from a plain program's by a relative error of at most 0.0026.
Values may be sent and summed in bfloat16 or wider, within the bound.
No kernel may reach another device: no remote copies, remote signals or barrier semaphores. Data moves between devices by JAX's collectives and lax.ppermute only.
A program may use at most 64 MiB of HBM per device.

v0:
```python
import jax
import jax.numpy as jnp
from jax import lax
from jax.sharding import PartitionSpec as P

BS = 64


def with_halo(cells, sides, width):
    for axis, dim in sides:
        count = lax.axis_size(axis)
        ends = count - 1
        head = lax.slice_in_dim(cells, 0, width, axis=dim)
        tail = lax.slice_in_dim(cells, cells.shape[dim] - width, cells.shape[dim], axis=dim)
        cells = jnp.concatenate(
            [
                lax.ppermute(tail, axis, [(i, (i + 1) % count) for i in range(ends)]),
                cells,
                lax.ppermute(head, axis, [((i + 1) % count, i) for i in range(ends)]),
            ],
            axis=dim,
        )
    return cells


def block_rows(image):
    visits, height, tile_width = image.shape
    pieces = image.reshape(visits, height // BS, BS, tile_width // BS, BS)
    return jnp.transpose(pieces, (0, 1, 3, 2, 4)).reshape(-1, BS * BS)


def shards(
    science,
    inverse_variance,
    template,
    filters,
    kernel_index,
    spatial_coeff,
    visit_offset,
    block_count,
    block_owner,
    block_slot,
    coadd_sum,
    coadd_weight,
):
    tile_count = lax.axis_size("tile")
    own_tile = template[0, 0]
    height, tile_width = own_tile.shape
    visits = science.shape[2]
    offsets = visit_offset[0]
    strips = own_tile.reshape(tile_count, height // tile_count, tile_width)
    held_strips = lax.all_to_all(strips, "tile", split_axis=0, concat_axis=0, tiled=True)
    outgoing = jnp.stack([jnp.roll(held_strips, -offsets[v], axis=0) for v in range(visits)])
    arrived = lax.all_to_all(outgoing, "tile", split_axis=1, concat_axis=1, tiled=True)
    aligned = arrived.reshape(visits, height, tile_width)
    basis_count, tap_total = filters.shape
    half_width = tap_total // 2
    kernel_total = kernel_index.shape[0]
    taps_all = filters.astype(jnp.float32)
    block_width = min(128, tile_width)
    block_total = tile_width // block_width
    window_width = block_width + 2 * half_width
    window_pos = lax.broadcasted_iota(jnp.int32, (window_width, block_width), 0)
    output_pos = lax.broadcasted_iota(jnp.int32, (window_width, block_width), 1)
    tap_offset = window_pos - output_pos
    band_table = jnp.zeros((window_width, basis_count, block_width), jnp.float32)
    for q in range(tap_total):
        band_table = band_table + jnp.where(
            (tap_offset == q)[:, None, :], taps_all[None, :, q, None], 0.0
        )
    band_table = band_table.astype(jnp.bfloat16)
    padded = jnp.pad(
        aligned.reshape(visits * height, tile_width), ((0, 0), (half_width, half_width))
    )
    windows = jnp.stack(
        [padded[:, b * block_width : b * block_width + window_width] for b in range(block_total)],
        axis=1,
    )
    filtered = jnp.einsum("rbq,qjx->rjbx", windows, band_table, preferred_element_type=jnp.float32)
    filtered = filtered.astype(jnp.bfloat16).reshape(visits, height, basis_count, tile_width)
    basis_ids = jnp.arange(basis_count, dtype=jnp.int32)
    row_pick = (kernel_index[:, 0, None] == basis_ids[None, :]).astype(jnp.bfloat16)
    column_pick = (kernel_index[:, 1, None] == basis_ids[None, :]).astype(jnp.float32)
    column_taps = jnp.dot(
        column_pick, taps_all, precision=lax.Precision.HIGHEST, preferred_element_type=jnp.float32
    )
    target_row = lax.broadcasted_iota(jnp.int32, (height, height), 0)
    source_row = lax.broadcasted_iota(jnp.int32, (height, height), 1)
    row_offset = source_row - target_row + half_width
    column_band = jnp.zeros((kernel_total, height, height), jnp.float32)
    for p in range(tap_total):
        column_band = column_band + jnp.where(
            (row_offset == p)[None, :, :], column_taps[:, p, None, None], 0.0
        )
    across = (2.0 * jnp.arange(tile_width, dtype=jnp.float32) + 1.0 - tile_width) / tile_width
    downward = (2.0 * jnp.arange(height, dtype=jnp.float32) + 1.0 - height) / height
    band_stack = jnp.concatenate([column_band, downward[None, :, None] * column_band], axis=0)
    selected = jnp.einsum("kj,vhjw->vkhw", row_pick, filtered, preferred_element_type=jnp.float32)
    coeffs = spatial_coeff[0, 0]
    column_weight = coeffs[:, 0, :, None] + coeffs[:, 1, :, None] * across[None, None, :]
    operand_stack = jnp.concatenate(
        [selected * column_weight[:, :, None, :], selected * coeffs[:, 2, :, None, None]], axis=1
    )
    matched = jnp.einsum(
        "kyg,vkgw->vyw",
        band_stack,
        operand_stack,
        precision=lax.Precision.HIGHEST,
        preferred_element_type=jnp.float32,
    )
    difference = science[0, 0] - matched
    inverse = inverse_variance[0, 0].astype(jnp.float32)
    blocks_per_visit = height // BS * (tile_width // BS)
    row_total = visits * blocks_per_visit
    weighted = block_rows(inverse * difference)
    weight_rows = block_rows(inverse)
    row_index = jnp.arange(row_total, dtype=jnp.int32)
    limits = jnp.repeat(block_count[0, 0], blocks_per_visit)
    is_valid = row_index % blocks_per_visit < limits
    row_mask = is_valid.astype(jnp.float32)
    payload = jnp.concatenate([weighted, weight_rows], axis=1) * row_mask[:, None]
    owners = block_owner[0, 0]
    patch_slot = block_slot[0, 0]
    patch_count = coadd_sum.shape[2]
    destination = owners * patch_count + patch_slot
    wanted = lax.broadcasted_iota(jnp.int32, (patch_count * lax.axis_size("tile"), row_total), 0)
    picker = (wanted == destination[None, :]).astype(jnp.float32)
    patches = lax.psum_scatter(
        jnp.dot(
            picker, payload, precision=lax.Precision.HIGHEST, preferred_element_type=jnp.float32
        ),
        "tile",
        scatter_dimension=0,
        tiled=True,
    )
    stacked = patches.reshape(patch_count, 2, -1)
    widened = with_halo(stacked, (("sky", 0),), 1)
    merged = stacked.at[0].add(widened[0]).at[-1].add(widened[-1])
    result = (coadd_sum[0, 0] + merged[:, 0]) / (coadd_weight[0, 0] + merged[:, 1])
    return (difference[None, None], result[None, None])


def solution(mesh):
    return jax.shard_map(
        shards,
        mesh=mesh,
        in_specs=(
            P("sky", "tile", None, None, None),
            P("sky", "tile", None, None, None),
            P("sky", "tile", None, None),
            P(),
            P(),
            P("sky", "tile", None, None, None),
            P("sky", None),
            P("sky", "tile", None),
            P("sky", "tile", None),
            P("sky", "tile", None),
            P("sky", "tile", None, None),
            P("sky", "tile", None, None),
        ),
        out_specs=(P("sky", "tile", None, None, None), P("sky", "tile", None, None)),
        check_vma=False,
    )
```

profile of v0, /device:TPU:102, one launch (start us, length us, event | category | flops | bytes accessed | tf_op | source)
XLA Modules:
  0.0 272.2 jit_solution(8171609969449274356)
XLA Ops:
  7.2 1.6 reshape_squeeze.3
  8.8 7.6 %all-to-all-start = ((bf16[32,4,512]{2,1,0:T(4,128)(2,1)}), bf16[32,4,512]{2,1,0:T(4,128)(2,1)S(1)}, u32[]{:S(2)}, u32[]{:S(2)}) async-start(bf16[32,4,512]{2,1,0:T(4,128)(2,1)} %reshape_squeeze.3), calls=%async_computation | async-start | bytes 262144 | tf_op jit(solution)/shard_map/all_to_all | solution.py:52
  19.9 1.3 slice_bitcast_fusion.8
  21.2 0.9 fusion.116
  25.8 6.2 %broadcast_multiply_fusion = (f32[20,128,128]{1,0,2:T(8,128)}, f32[20,128,128]{1,0,2:T(8,128)}) fusion(f32[128]{0:T(128)S(1)} %add_multiply_fusion.1, f32[20]{0:T(128)S(1)} %get-tuple-element.36, pred[128,128]{0,1:T(8,128)(4,1)S(1)} %get-tuple-element.96, f32[20]{0:T(128)S(1)} %get-tuple-element.37, pred[128,128]{0,1:T(8,128)(4,1)S(1)} %get-tuple-element.97, ...), kind=kLoop, calls=%fused_computation.16 | loop fusion | flops 13762560 | bytes 2967696 | tf_op jit(solution)/shard_map/mul | solution.py:97
  34.0 1.0 slice_reduce_fusion.41
  35.3 0.9 pad_maximum_fusion
  36.2 7.4 %all-to-all-start.1 = ((bf16[2,32,4,512]{3,2,0,1:T(4,128)(2,1)}), bf16[2,32,4,512]{3,2,0,1:T(4,128)(2,1)S(1)}, u32[]{:S(2)}, u32[]{:S(2)}) async-start(bf16[2,32,4,512]{3,2,0,1:T(4,128)(2,1)} %pad_maximum_fusion), calls=%async_computation.1 | async-start | bytes 524288 | tf_op jit(solution)/shard_map/all_to_all | solution.py:54
  44.6 1.0 copy.35
  47.5 3.1 %all-to-all-done.1 = bf16[2,32,4,512]{3,2,0,1:T(4,128)(2,1)S(1)} async-done(((bf16[2,32,4,512]{3,2,0,1:T(4,128)(2,1)}), bf16[2,32,4,512]{3,2,0,1:T(4,128)(2,1)S(1)}, u32[]{:S(2)}, u32[]{:S(2)}) %all-to-all-start.1) | async-done | bytes 262176 | tf_op jit(solution)/shard_map/all_to_all | solution.py:54
  51.0 3.1 %convert_bitcast_fusion = bf16[256,8,4,128]{0,3,2,1:T(8,128)(2,1)S(1)} fusion(bf16[256,1,148]{0,2,1:T(8,128)(2,1)S(1)} %get-tuple-element.82, bf16[256,1,148]{0,2,1:T(8,128)(2,1)S(1)} %get-tuple-element.83, bf16[256,1,148]{0,2,1:T(8,128)(2,1)S(1)} %get-tuple-element.84, bf16[256,1,148]{0,2,1:T(8,128)(2,1)S(1)} %get-tuple-element.81, ...), kind=kOutput, calls=%fused_computation.9 | convolution fusion | flops 319004672 | bytes 2798752 | tf_op jit(solution)/shard_map/rbq,qjx->rjbx/dot_general | solution.py:79
  54.1 2.1 reshape.406
  56.2 3.6 %copy.40 = bf16[2,128,8,512]{3,2,1,0:T(8,128)(2,1)S(1)} copy(bf16[2,128,8,512]{1,0,3,2:T(2,128)(2,1)} %reshape.406) | data formatting | bytes 4194304 | tf_op jit(solution)/shard_map/reshape | solution.py:80
  59.8 6.5 %bitcast_multiply_fusion.1 = (f32[2,20,128,512]{3,1,2,0:T(8,128)S(1)}, f32[2,20,128,512]{3,1,2,0:T(8,128)}) fusion(f32[2,20,512]{2,1,0:T(8,128)S(1)} %multiply_add_fusion, f32[2,20]{1,0:T(2,128)S(1)} %get-tuple-element.88, bf16[2,128,8,512]{3,2,1,0:T(8,128)(2,1)S(1)} %copy.40, s32[20]{0:T(128)S(1)} %copy-done.11), kind=kOutput, calls=%fused_computation.5 | convolution fusion | flops 47186080 | bytes 23150832 | tf_op jit(solution)/shard_map/kj,vhjw->vkhw/dot_general | solution.py:98
  66.3 36.5 %bitcast_multiply_fusion.2 = (f32[2,128,512]{1,2,0:T(8,128)S(1)}, f32[2,128,512]{1,2,0:T(8,128)S(1)}) fusion(bf16[1,1,2,128,512]{3,4,2,1,0:T(8,128)(2,1)S(1)} %copy.41, f32[20,128,128]{1,0,2:T(8,128)S(1)} %copy-done, f32[20,128,128]{1,0,2:T(8,128)S(1)} %copy-done.1, f32[2,20,128,512]{3,1,2,0:T(8,128)} %get-tuple-element.80, ...), kind=kOutput, calls=%fused_computation.19 | convolution fusion | flops 8059355136 | bytes 25427968 | tf_op jit(solution)/shard_map/kyg,vkgw->vyw/dot_general | solution.py:104
  104.4 3.2 %fusion.9 = f32[96,8192]{1,0:T(8,128)} fusion(f32[32,4096]{1,0:T(8,128)S(1)} %reshape.416, f32[32,4096]{1,0:T(8,128)S(1)} %reshape.408, f32[32]{0:T(128)S(1)} %copy-done.13, s32[32]{0:T(128)S(1)} %copy-done.14), kind=kOutput, calls=%fused_computation.13 | convolution fusion | flops 302517248 | bytes 4194560 | tf_op jit(solution)/shard_map/dot_general | solution.py:129
  107.6 1.3 dynamic-slice.14
  109.5 1.0 copy.46
  110.5 139.9 %all-reduce.4.cloned.1.call-done = f32[96,8192]{1,0:T(8,128)} async-done(((f32[96,8192]{1,0:T(8,128)}), f32[96,8192]{1,0:T(8,128)}) %all-reduce.4.cloned.1.call-update) | async-done | bytes 3145744
  250.4 1.2 dynamic-slice_reduce_fusion
  251.7 4.7 %collective-permute-start = (f32[1,2,4096]{2,1,0:T(2,128)S(1)}, f32[1,2,4096]{2,1,0:T(2,128)S(1)}, u32[]{:S(2)}, u32[]{:S(2)}) collective-permute-start(f32[1,2,4096]{2,1,0:T(2,128)S(1)} %slice.277), channel_id=1, source_target_pairs={{0,32},{32,64},{64,96},{96,128},{128,160},{160,192},{192,224},{224... | collective-permute-start | bytes 98312 | tf_op jit(solution)/shard_map/ppermute | solution.py:17
  256.3 1.1 constant_dynamic-slice_fusion
  257.6 1.9 collective-permute-start.1
  259.5 5.0 %collective-permute-done.1 = f32[1,2,4096]{2,1,0:T(2,128)S(1)} collective-permute-done((f32[1,2,4096]{2,1,0:T(2,128)S(1)}, f32[1,2,4096]{2,1,0:T(2,128)S(1)}, u32[]{:S(2)}, u32[]{:S(2)}) %collective-permute-start.1) | collective-permute-done | bytes 32800 | tf_op jit(solution)/shard_map/ppermute | solution.py:19
  (95 shorter events, 13.7 us)
Async XLA Ops:
  7.2 16.7 %copy-start.10 = (f32[1,1,2,3,20]{4,2,3,1,0:T(2,128)S(1)}, f32[1,1,2,3,20]{4,2,3,1,0:T(2,128)}, u32[]{:S(2)}) copy-start(f32[1,1,2,3,20]{4,2,3,1,0:T(2,128)} %param.23) | copy-start | bytes 1444
  7.2 17.3 %copy-start.15 = (s32[1,1,2]{2,1,0:T(1,128)S(1)}, s32[1,1,2]{2,1,0:T(1,128)}, u32[]{:S(2)}) copy-start(s32[1,1,2]{2,1,0:T(1,128)} %param.25) | copy-start | bytes 28
  7.2 18.0 %copy-start.17 = (s32[1,1,32]{2,1,0:T(1,128)S(1)}, s32[1,1,32]{2,1,0:T(1,128)}, u32[]{:S(2)}) copy-start(s32[1,1,32]{2,1,0:T(1,128)} %param.26) | copy-start | bytes 388
  7.2 18.0 %copy-start.16 = (s32[1,1,32]{2,1,0:T(1,128)S(1)}, s32[1,1,32]{2,1,0:T(1,128)}, u32[]{:S(2)}) copy-start(s32[1,1,32]{2,1,0:T(1,128)} %param.27) | copy-start | bytes 388
  8.8 26.3 %all-to-all-start = ((bf16[32,4,512]{2,1,0:T(4,128)(2,1)}), bf16[32,4,512]{2,1,0:T(4,128)(2,1)S(1)}, u32[]{:S(2)}, u32[]{:S(2)}) async-start(bf16[32,4,512]{2,1,0:T(4,128)(2,1)} %reshape_squeeze.3), calls=%async_computation | async-start | bytes 262144 | tf_op jit(solution)/shard_map/all_to_all | solution.py:52
  25.8 6.2 %copy-start.12 = (s32[1,2]{1,0:T(1,128)S(1)}, s32[1,2]{1,0:T(1,128)}, u32[]{:S(2)}) copy-start(s32[1,2]{1,0:T(1,128)} %param.24) | copy-start | bytes 28
  32.0 12.5 %copy-start.4 = (bf16[1,1,2,128,512]{4,3,2,1,0:T(8,128)(2,1)S(1)}, bf16[1,1,2,128,512]{4,3,2,1,0:T(8,128)(2,1)}, u32[]{:S(2)}) copy-start(bf16[1,1,2,128,512]{4,3,2,1,0:T(8,128)(2,1)} %param.19) | copy-start | bytes 786436
  32.0 12.6 %copy-start.2 = (f32[1,1,2,128,512]{4,3,2,1,0:T(8,128)S(1)}, f32[1,1,2,128,512]{4,3,2,1,0:T(8,128)}, u32[]{:S(2)}) copy-start(f32[1,1,2,128,512]{4,3,2,1,0:T(8,128)} %param.18) | copy-start | bytes 1572868
  36.2 14.4 %all-to-all-start.1 = ((bf16[2,32,4,512]{3,2,0,1:T(4,128)(2,1)}), bf16[2,32,4,512]{3,2,0,1:T(4,128)(2,1)S(1)}, u32[]{:S(2)}, u32[]{:S(2)}) async-start(bf16[2,32,4,512]{3,2,0,1:T(4,128)(2,1)} %pad_maximum_fusion), calls=%async_computation.1 | async-start | bytes 524288 | tf_op jit(solution)/shard_map/all_to_all | solution.py:54
  43.6 206.8 %all-reduce.4.cloned.1.call-start = ((), (), s32[]{:S(2)}) async-start(), calls=%async_computation.2 | async-start | bytes 6291456
  46.7 0.7 copy-start.7
  46.7 0.7 copy-start.8
  46.7 0.7 copy-start.9
  56.2 3.6 %copy-start.11 = (s32[20]{0:T(128)S(1)}, s32[20]{0:T(128)}, u32[]{:S(2)}) copy-start(s32[20]{0:T(128)} %get-tuple-element.90) | copy-start | bytes 244
  59.7 6.5 %copy-start = (f32[20,128,128]{1,0,2:T(8,128)S(1)}, f32[20,128,128]{1,0,2:T(8,128)}, u32[]{:S(2)}) copy-start(f32[20,128,128]{1,0,2:T(8,128)} %get-tuple-element.77) | copy-start | bytes 3932164
  59.7 6.5 %copy-start.1 = (f32[20,128,128]{1,0,2:T(8,128)S(1)}, f32[20,128,128]{1,0,2:T(8,128)}, u32[]{:S(2)}) copy-start(f32[20,128,128]{1,0,2:T(8,128)} %get-tuple-element.78) | copy-start | bytes 3932164
  59.7 6.5 %copy-start.3 = (f32[1,1,2,128,512]{3,4,2,1,0:T(8,128)S(1)}, f32[1,1,2,128,512]{3,4,2,1,0:T(8,128)}, u32[]{:S(2)}) copy-start(f32[1,1,2,128,512]{3,4,2,1,0:T(8,128)} %copy.35) | copy-start | bytes 1572868
  103.4 0.9 copy-start.13
  103.5 0.9 copy-start.14
  107.5 157.1 %copy-start.5 = (f32[1,1,3,4096]{3,1,2,0:T(1,128)S(1)}, f32[1,1,3,4096]{3,1,2,0:T(1,128)}, u32[]{:S(2)}) copy-start(f32[1,1,3,4096]{3,1,2,0:T(1,128)} %param.29) | copy-start | bytes 147460
  107.6 157.1 %copy-start.6 = (f32[1,1,3,4096]{3,1,2,0:T(1,128)S(1)}, f32[1,1,3,4096]{3,1,2,0:T(1,128)}, u32[]{:S(2)}) copy-start(f32[1,1,3,4096]{3,1,2,0:T(1,128)} %param.28) | copy-start | bytes 147460
  251.7 7.8 %collective-permute-start = (f32[1,2,4096]{2,1,0:T(2,128)S(1)}, f32[1,2,4096]{2,1,0:T(2,128)S(1)}, u32[]{:S(2)}, u32[]{:S(2)}) collective-permute-start(f32[1,2,4096]{2,1,0:T(2,128)S(1)} %slice.277), channel_id=1, source_target_pairs={{0,32},{32,64},{64,96},{96,128},{128,160},{160,192},{192,224},{224... | collective-permute-start | bytes 98312 | tf_op jit(solution)/shard_map/ppermute | solution.py:17
  257.6 7.0 %collective-permute-start.1 = (f32[1,2,4096]{2,1,0:T(2,128)S(1)}, f32[1,2,4096]{2,1,0:T(2,128)S(1)}, u32[]{:S(2)}, u32[]{:S(2)}) collective-permute-start(f32[1,2,4096]{2,1,0:T(2,128)S(1)} %reshape.413), channel_id=1, source_target_pairs={{32,0},{64,32},{96,64},{128,96},{160,128},{192,160},{224,192},{256... | collective-permute-start | bytes 98312 | tf_op jit(solution)/shard_map/ppermute | solution.py:19
Sparse Core Ops, SparseCore 0:
  107.7 142.6 all-reduce.3
where the time goes:
time: 273 us; the launch traced here: 272 us
  waiting for transfers between devices  148 us (54%)
  matrix products  50.1 us (18%)
  local copies, waits for them, and re-layouts  22.2 us (8%)
  starting transfers between devices  21.8 us (8%)
  between operations  16.6 us (6%)
  other arithmetic  13.4 us (5%)
    unnamed x2, waiting for transfers between devices  140 us
    dot_general x1, matrix products, shards(): jnp.einsum('kyg,vkgw->vyw', band_stack, operand_stack, precision=lax.Prec...  36.5 us
    all_to_all x1, starting transfers between devices, shards(): lax.all_to_all(strips, 'tile', split_axis=0, concat_axis=0, tiled=True)  7.57 us
    all_to_all x1, starting transfers between devices, shards(): lax.all_to_all(outgoing, 'tile', split_axis=1, concat_axis=1, tiled=True)  7.38 us
    dot_general x1, matrix products, shards(): jnp.einsum('kj,vhjw->vkhw', row_pick, filtered, preferred_element_type=jn...  6.51 us
    mul x1, other arithmetic, shards(): downward[None, :, None] * column_band  6.18 us
    reshape x2, local copies, waits for them, and re-layouts, shards(): filtered.astype(jnp.bfloat16)  5.65 us
  transfers between devices with their start and end apart: 5, of which 3 were waited for; matrix products, arithmetic and copies ran while one was open for 9% of the time, Pallas kernels for 0%

commit v1 on v0

v1 whole, which is shorter than its diff:
```python
import jax
import jax.numpy as jnp
from jax import lax
from jax.experimental import pallas as pl
from jax.experimental.pallas import tpu as pltpu
from jax.sharding import PartitionSpec as P

TILES = 32
VISITS = 2
H = 128
W = 512
BS = 64
NB = 8
TAPS = 21
HALF = 10
LANE = 128
CB = W // LANE
NBLK = 32
PATCHES = 3
f32 = jnp.float32
bf16 = jnp.bfloat16
VMEM = pl.BlockSpec(memory_space=pltpu.VMEM)
SMEM = pl.BlockSpec(memory_space=pltpu.SMEM)


def call(kernel, outs, in_specs, cost, scratch=()):
    return pl.pallas_call(
        kernel,
        out_shape=outs,
        in_specs=in_specs,
        out_specs=jax.tree.map(lambda _: VMEM, outs),
        scratch_shapes=list(scratch),
        compiler_params=pltpu.CompilerParams(vmem_limit_bytes=48 * 2**20),
        cost_estimate=pl.CostEstimate(flops=cost[0], bytes_accessed=cost[1], transcendentals=0),
    )


def toeplitz(row, width):
    return pltpu.roll(jnp.broadcast_to(row, (LANE, width)), 0, 1, stride=1, stride_axis=0)


def prep_kernel(taps_ref, eff_ref, band_ref, hi_ref, lo_ref):
    for j in range(NB):
        band_ref[pl.ds(j * LANE, LANE), :] = toeplitz(taps_ref[j : j + 1, :], 2 * LANE).astype(bf16)
    row = lax.broadcasted_iota(jnp.int32, (H, H), 0)
    col = lax.broadcasted_iota(jnp.int32, (H, H), 1)
    inside = jnp.abs(row - col) <= HALF
    down = (2.0 * row.astype(f32) + 1.0 - H) / H
    for v in range(VISITS):
        for r in range(NB):
            base = v * 3 * NB + r
            parts = [toeplitz(eff_ref[base + t * NB : base + t * NB + 1, :], H) for t in range(3)]
            for m, value in enumerate((parts[0] + down * parts[2], parts[1])):
                value = jnp.where(inside, value, 0.0)
                high = value.astype(bf16)
                where = (v, pl.ds(m * H, H), pl.ds(r * H, H))
                hi_ref[where] = high
                lo_ref[where] = (value - high.astype(f32)).astype(bf16)


def roll_kernel(offset_ref, held_ref, out_ref):
    for v in range(VISITS):
        offset = offset_ref[0, v]
        for i in range(TILES):
            out_ref[i, pl.ds(v * 16, 16), :] = held_ref[(offset + i) & (TILES - 1)]


def main_kernel(
    place_ref, slot_ref, arrived_ref, band_ref, hi_ref, lo_ref, science_ref, inverse_ref,
    difference_ref, payload_ref, filtered_ref,
):
    payload_ref[...] = jnp.zeros_like(payload_ref)
    lane = lax.broadcasted_iota(jnp.int32, (H, LANE), 1)
    across = (2.0 * lax.broadcasted_iota(jnp.int32, (H, W), 1).astype(f32) + 1.0 - W) / W
    left = lax.broadcasted_iota(jnp.int32, (BS, LANE), 1) < BS
    left16 = lax.broadcasted_iota(jnp.int32, (16, LANE), 1) < BS
    zero = jnp.zeros((H, LANE), bf16)
    for v in range(VISITS):
        tiles = [
            jnp.concatenate(
                [arrived_ref[rb * CB + b, pl.ds(v * 16, 16), :] for rb in range(H // 16)], axis=0
            )
            for b in range(CB)
        ]
        for b in range(CB):
            after = tiles[b + 1] if b + 1 < CB else zero
            before = tiles[b - 1] if b > 0 else zero
            window = jnp.concatenate([tiles[b], jnp.where(lane < BS, after, before)], axis=1)
            rows = lax.dot_general(
                window, band_ref[...], (((1,), (1,)), ((), ())), preferred_element_type=f32
            ).astype(bf16)
            for j in range(NB):
                filtered_ref[pl.ds(j * H, H), pl.ds(b * LANE, LANE)] = rows[:, j * LANE : (j + 1) * LANE]
        filtered = filtered_ref[...]
        both = jnp.dot(hi_ref[v], filtered, preferred_element_type=f32) + jnp.dot(
            lo_ref[v], filtered, preferred_element_type=f32
        )
        difference = science_ref[v] - (both[:H] + across * both[H:])
        difference_ref[v] = difference
        inverse = inverse_ref[v].astype(f32)
        weighted = inverse * difference
        for by in range(H // BS):
            for pair in range(CB):
                cut = (slice(by * BS, (by + 1) * BS), slice(pair * LANE, (pair + 1) * LANE))
                straight, swapped = [], []
                for x in (weighted[cut], inverse[cut]):
                    straight.append(x.astype(bf16))
                    swapped.append(pltpu.roll(x, BS, 1).astype(bf16))
                straight = jnp.concatenate(straight, axis=0)
                swapped = jnp.concatenate(swapped, axis=0)
                for parity in range(2):
                    r = v * 16 + by * 8 + pair * 2 + parity
                    place = place_ref[r]
                    slot = slot_ref[r].astype(f32)

                    def put(half, data, place=place, slot=slot):
                        owner = place >> 1
                        keep = left if half == 0 else jnp.logical_not(left)
                        keep2 = jnp.concatenate([keep, keep], axis=0)
                        payload_ref[owner, pl.ds(0, 2 * BS), :] = jnp.where(
                            keep2, data, payload_ref[owner, pl.ds(0, 2 * BS), :]
                        )
                        keep16 = left16 if half == 0 else jnp.logical_not(left16)
                        payload_ref[owner, pl.ds(2 * BS, 16), :] = jnp.where(
                            keep16, jnp.full((16, LANE), slot).astype(bf16), payload_ref[owner, pl.ds(2 * BS, 16), :]
                        )

                    for half in range(2):
                        @pl.when(jnp.logical_and(place >= 0, (place & 1) == half))
                        def _(half=half):
                            put(half, straight if half == parity else swapped)


def sum_kernel(arrived_ref, total_ref):
    left = lax.broadcasted_iota(jnp.int32, (BS, LANE), 1) < BS
    sums = []
    for part in range(2):
        def body(j, acc):
            head = arrived_ref[j, pl.ds(2 * BS, 16), :].astype(f32)[:1]
            value = arrived_ref[j, pl.ds(part * BS, BS), :].astype(f32)
            return tuple(
                acc[s] + jnp.where(jnp.broadcast_to(head == s, (BS, LANE)), value, 0.0) for s in range(PATCHES)
            )
        acc = lax.fori_loop(0, TILES, body, tuple(jnp.zeros((BS, LANE), f32) for _ in range(PATCHES)), unroll=4)
        sums.append([a + pltpu.roll(a, BS, 1) for a in acc])
    for s in range(PATCHES):
        total_ref[s] = jnp.where(left, sums[0][s], sums[1][s])


def final_kernel(total_ref, low_ref, high_ref, sum_ref, weight_ref, out_ref, merged_ref):
    left = lax.broadcasted_iota(jnp.int32, (BS // 2, LANE), 1) < BS
    for s in range(PATCHES):
        merged = total_ref[s]
        if s == 0:
            merged = merged + low_ref[...]
        if s == PATCHES - 1:
            merged = merged + high_ref[...]
        merged_ref[...] = merged
        even = merged_ref[pl.ds(0, BS // 2, stride=2), :]
        odd = merged_ref[pl.ds(1, BS // 2, stride=2), :]
        value = jnp.where(left, even, pltpu.roll(odd, BS, 1))
        weight = jnp.where(left, pltpu.roll(even, BS, 1), odd)
        result = (sum_ref[s] + value) / (weight_ref[s] + weight)
        for i in range(BS // 2):
            out_ref[s : s + 1, pl.ds(i * LANE, LANE)] = result[i : i + 1, :]


def all_to_all(x):
    return lax.all_to_all(x, "tile", split_axis=0, concat_axis=0, tiled=True)


def shards(
    science,
    inverse_variance,
    template,
    filters,
    kernel_index,
    spatial_coeff,
    visit_offset,
    block_count,
    block_owner,
    block_slot,
    coadd_sum,
    coadd_weight,
):
    sds = jax.ShapeDtypeStruct
    strips = template[0, 0].reshape(H // 16, 16, CB, LANE).transpose(0, 2, 1, 3).reshape(TILES, 16, LANE)
    held = all_to_all(strips)

    taps = filters.astype(f32)
    ids = jnp.arange(NB, dtype=jnp.int32)
    row_pick = (kernel_index[:, 0, None] == ids[None, :]).astype(f32)
    column_pick = (kernel_index[:, 1, None] == ids[None, :]).astype(f32)
    column_taps = jnp.sum(column_pick[:, :, None] * taps[None], axis=1)
    coeffs = spatial_coeff[0, 0].reshape(VISITS * 3, -1)
    effective = jnp.sum(
        (coeffs[:, None, :] * row_pick.T[None])[..., None] * column_taps[None, None], axis=2
    ).reshape(VISITS * 3 * NB, TAPS)

    def centred(rows, width):
        gap = jnp.zeros((rows.shape[0], width - TAPS), f32)
        return jnp.concatenate([rows[:, HALF:], gap, rows[:, :HALF]], axis=1)

    band, hi, lo = call(
        prep_kernel,
        (
            sds((NB * LANE, 2 * LANE), bf16),
            sds((VISITS, 2 * H, NB * H), bf16),
            sds((VISITS, 2 * H, NB * H), bf16),
        ),
        [VMEM, VMEM],
        (10_000_000, 3_000_000),
    )(centred(taps, 2 * LANE), centred(effective, H))

    owners = block_owner[0, 0]
    row = jnp.arange(NBLK, dtype=jnp.int32)
    earlier = (owners[:, None] == owners[None, :]) & (row[None, :] < row[:, None])
    repeat = jnp.sum(earlier.astype(jnp.int32), axis=1)
    counted = row % (NBLK // VISITS) < jnp.repeat(block_count[0, 0], NBLK // VISITS)
    place = jnp.where(counted, 2 * owners + repeat, -1)

    outgoing = call(
        roll_kernel, sds((TILES, VISITS * 16, LANE), bf16), [SMEM, VMEM], (0, 400_000)
    )(visit_offset, held)
    arrived = all_to_all(outgoing)

    difference, payload = call(
        main_kernel,
        (sds((VISITS, H, W), f32), sds((TILES, 2 * BS + 16, LANE), bf16)),
        [SMEM, SMEM] + [VMEM] * 6,
        (2_000_000_000, 6_000_000),
        [pltpu.VMEM((NB * H, W), bf16)],
    )(place, block_slot[0, 0], arrived, band, hi, lo, science[0, 0], inverse_variance[0, 0])

    total = call(
        sum_kernel, sds((PATCHES, BS, LANE), f32), [VMEM], (10_000_000, 1_300_000)
    )(all_to_all(payload))

    count = lax.axis_size("sky")
    low = lax.ppermute(total[PATCHES - 1], "sky", [(i, i + 1) for i in range(count - 1)])
    high = lax.ppermute(total[0], "sky", [(i + 1, i) for i in range(count - 1)])
    result = call(
        final_kernel,
        sds((PATCHES, BS * BS), f32),
        [VMEM] * 5,
        (100_000, 300_000),
        [pltpu.VMEM((BS, LANE), f32)],
    )(
        total,
        low,
        high,
        coadd_sum[0, 0].reshape(PATCHES, BS // 2, LANE),
        coadd_weight[0, 0].reshape(PATCHES, BS // 2, LANE),
    )
    return (difference[None, None], result[None, None])


def solution(mesh):
    return jax.shard_map(
        shards,
        mesh=mesh,
        in_specs=(
            P("sky", "tile", None, None, None),
            P("sky", "tile", None, None, None),
            P("sky", "tile", None, None),
            P(),
            P(),
            P("sky", "tile", None, None, None),
            P("sky", None),
            P("sky", "tile", None),
            P("sky", "tile", None),
            P("sky", "tile", None),
            P("sky", "tile", None, None),
            P("sky", "tile", None, None),
        ),
        out_specs=(P("sky", "tile", None, None, None), P("sky", "tile", None, None)),
        check_vma=False,
    )
```

time: 273 us -> 74.6 us (0.27)
  the two profiles are of different devices: /device:TPU:102 before, /device:TPU:384 now
where the time goes in v1:
time: 74.6 us; the launch traced here: 74.1 us
  blocking collectives  22.5 us (30%)
  starting transfers between devices  17.5 us (23%)
  waiting for transfers between devices  15.1 us (20%)
  Pallas kernels  9.15 us (12%)
  local copies, waits for them, and re-layouts  7.5 us (10%)
  other arithmetic  1.53 us (2%)
  between operations  0.82 us (1%)
    all_to_all x1, blocking collectives, all_to_all(): return lax.all_to_all(x, 'tile', split_axis=0, concat_axis=0, tiled=True)  22.5 us
    all_to_all x2, starting transfers between devices, all_to_all(): return lax.all_to_all(x, 'tile', split_axis=0, concat_axis=0, tiled=True)  11.4 us
    all_to_all x2, waiting for transfers between devices, all_to_all(): return lax.all_to_all(x, 'tile', split_axis=0, concat_axis=0, tiled=True)  9.97 us
    pallas_call x1, Pallas kernels, shards(): call(main_kernel, (sds((VISITS, H, W), f32), sds((TILES, 2 * BS + 16, LAN...  5.78 us
    ppermute x1, waiting for transfers between devices, shards(): lax.ppermute(total[PATCHES - 1], 'sky', [(i, i + 1) for i in range(count...  5.08 us
    ppermute x1, starting transfers between devices, shards(): high = lax.ppermute(total[0], 'sky', [(i + 1, i) for i in range(count - 1)])  4.17 us
    unnamed x22, local copies, waits for them, and re-layouts  3.21 us
    ppermute x1, starting transfers between devices, shards(): lax.ppermute(total[PATCHES - 1], 'sky', [(i, i + 1) for i in range(count...  1.92 us
  transfers between devices with their start and end apart: 4, of which 3 were waited for; matrix products, arithmetic and copies ran while one was open for 6% of the time, Pallas kernels for 1%

profile of v1, /device:TPU:384, one launch (start us, length us, event | category | flops | bytes accessed | tf_op | source)
XLA Modules:
  0.0 74.1 jit_solution(12645887484138436826)
XLA Ops:
  0.7 1.0 %reshape_squeeze.9 = bf16[8,16,4,128]{3,2,1,0:T(4,128)(2,1)S(1)} reshape(bf16[1,1,128,512]{3,2,1,0:T(8,128)(2,1)} %param.14) | data formatting | bytes 262144 | tf_op jit(solution)/shard_map/reshape;squeeze | solution.py:187
  1.7 0.7 copy.20
  2.4 7.3 %all-to-all-start = ((bf16[32,16,128]{2,1,0:T(8,128)(2,1)}), bf16[32,16,128]{2,1,0:T(8,128)(2,1)S(1)}, u32[]{:S(2)}, u32[]{:S(2)}) async-start(bf16[32,16,128]{2,1,0:T(8,128)(2,1)} %bitcast.4), calls=%async_computation | async-start | bytes 262144 | tf_op jit(solution)/shard_map/all_to_all | solution.py:169
  9.7 0.8 %slice.26 = f32[8,11]{1,0:T(8,128)S(1)} slice(bf16[8,21]{1,0:T(8,128)(2,1)} %param.15), slice={[0:8], [10:21]} | slice | bytes 704 | tf_op jit(solution)/shard_map/slice | solution.py:202
  10.5 0.7 slice.27
  11.2 0.7 convert_element_type.22
  12.0 0.8 %slice_bitcast_fusion.3 = (s32[20]{0:T(128)S(1)}, s32[20]{0:T(128)S(1)}) fusion(s32[20,2]{0,1:T(2,128)} %param.16), kind=kLoop, calls=%fused_computation.17 | loop fusion | bytes 320 | tf_op jit(solution)/shard_map/eq | solution.py:192
  12.8 0.7 copy.21
  13.8 0.2 multiply_reduce_fusion
  14.2 3.3 %all-to-all-done.held_ref = bf16[32,16,128]{2,1,0:T(8,128)(2,1)S(1)} async-done(((bf16[32,16,128]{2,1,0:T(8,128)(2,1)}), bf16[32,16,128]{2,1,0:T(8,128)(2,1)S(1)}, u32[]{:S(2)}, u32[]{:S(2)}) %all-to-all-start) | async-done | bytes 131104 | tf_op jit(solution)/shard_map/all_to_all | solution.py:169
  17.5 1.3 %shard_map.131 = bf16[32,32,128]{2,1,0:T(8,128)(2,1)} custom-call(s32[1,2]{1,0:T(1,128)S(1)} %copy-done.2, bf16[32,16,128]{2,1,0:T(8,128)(2,1)S(1)} %all-to-all-done.held_ref), custom_call_target="tpu_custom_call" | custom-call | bytes 400000 | tf_op jit(solution)/shard_map/pallas_call | solution.py:222
  18.8 4.1 %all-to-all-start.1 = ((bf16[32,32,128]{2,1,0:T(8,128)(2,1)}), bf16[32,32,128]{2,1,0:T(8,128)(2,1)S(1)}, u32[]{:S(2)}, u32[]{:S(2)}) async-start(bf16[32,32,128]{2,1,0:T(8,128)(2,1)} %shard_map.131), calls=%async_computation.1 | async-start | bytes 524288 | tf_op jit(solution)/shard_map/all_to_all | solution.py:169
  22.9 0.2 convert_reduce_fusion
  23.3 1.1 %shard_map.132 = (bf16[1024,256]{1,0:T(8,128)(2,1)S(1)}, bf16[2,256,1024]{2,1,0:T(8,128)(2,1)S(1)}, bf16[2,256,1024]{2,1,0:T(8,128)(2,1)S(1)}) custom-call(f32[8,256]{1,0:T(8,128)S(1)} %pad_maximum_fusion.1.taps_ref, f32[48,128]{1,0:T(8,128)S(1)} %pad_maximum_fusion.eff_ref), custom_call_target="tpu_custom_call" | custom-call | flops 10000000 | bytes 3000000 | tf_op jit(solution)/shard_map/pallas_call | solution.py:204
  24.4 0.8 %copy-done.6 = bf16[1024,256]{1,0:T(8,128)(2,1)} copy-done((bf16[1024,256]{1,0:T(8,128)(2,1)}, bf16[1024,256]{1,0:T(8,128)(2,1)S(1)}, u32[]{:S(2)}) %copy-start.6) | copy-done | bytes 524312
  25.2 6.7 %all-to-all-done.1.arrived_ref = bf16[32,32,128]{2,1,0:T(8,128)(2,1)S(1)} async-done(((bf16[32,32,128]{2,1,0:T(8,128)(2,1)}), bf16[32,32,128]{2,1,0:T(8,128)(2,1)S(1)}, u32[]{:S(2)}, u32[]{:S(2)}) %all-to-all-start.1) | async-done | bytes 262176 | tf_op jit(solution)/shard_map/all_to_all | solution.py:169
  31.9 1.0 %copy-done.7 = bf16[1024,256]{1,0:T(8,128)(2,1)S(1)} copy-done((bf16[1024,256]{1,0:T(8,128)(2,1)S(1)}, bf16[1024,256]{1,0:T(8,128)(2,1)}, u32[]{:S(2)}) %copy-start.7) | copy-done | bytes 524312
  32.9 5.8 %shard_map.133 = (f32[2,128,512]{2,1,0:T(8,128)}, bf16[32,144,128]{2,1,0:T(8,128)(2,1)S(1)}) custom-call(s32[32]{0:T(128)S(1)} %compare_select_fusion.place_ref, s32[32]{0:T(128)S(1)} %bitcast.30, bf16[32,32,128]{2,1,0:T(8,128)(2,1)S(1)} %all-to-all-done.1.arrived_ref, bf16[1024,256]{1,0:T(8,128)(2,1)S(1)} %copy-done.7, ...), custom_call_target="tpu_custom_call" | custom-call | flops 2000000000 | bytes 6000000 | tf_op jit(solution)/shard_map/pallas_call | solution.py:227
  38.7 22.5 %all_to_all.15.arrived_ref = bf16[32,144,128]{2,1,0:T(8,128)(2,1)S(1)} all-to-all(bf16[32,144,128]{2,1,0:T(8,128)(2,1)S(1)} %get-tuple-element.11), channel_id=1, replica_groups=mesh['sky'=16,'tile'=32] {'tile'}, dimensions={0} | all-to-all | bytes 2359296 | tf_op jit(solution)/shard_map/all_to_all | solution.py:169
  61.2 0.9 %shard_map.134.total_ref = f32[3,64,128]{2,1,0:T(8,128)S(1)} custom-call(bf16[32,144,128]{2,1,0:T(8,128)(2,1)S(1)} %all_to_all.15.arrived_ref), custom_call_target="tpu_custom_call" | custom-call | flops 10000000 | bytes 1300000 | tf_op jit(solution)/shard_map/pallas_call | solution.py:235
  62.1 4.2 %collective-permute-start.1 = (f32[64,128]{1,0:T(8,128)S(1)}, f32[64,128]{1,0:T(8,128)S(1)}, u32[]{:S(2)}, u32[]{:S(2)}) collective-permute-start(f32[64,128]{1,0:T(8,128)S(1)} %get-tuple-element.18), channel_id=1, source_target_pairs={{32,0},{64,32},{96,64},{128,96},{160,128},{192,160},{224,192},{256... | collective-permute-start | bytes 98312 | tf_op jit(solution)/shard_map/ppermute | solution.py:241
  66.3 1.9 %collective-permute-start = (f32[64,128]{1,0:T(8,128)S(1)}, f32[64,128]{1,0:T(8,128)S(1)}, u32[]{:S(2)}, u32[]{:S(2)}) collective-permute-start(f32[64,128]{1,0:T(8,128)S(1)} %get-tuple-element.19), channel_id=1, source_target_pairs={{0,32},{32,64},{64,96},{96,128},{128,160},{160,192},{192,224},{224... | collective-permute-start | bytes 98312 | tf_op jit(solution)/shard_map/ppermute | solution.py:240
  68.2 5.1 %collective-permute-done.low_ref = f32[64,128]{1,0:T(8,128)S(1)} collective-permute-done((f32[64,128]{1,0:T(8,128)S(1)}, f32[64,128]{1,0:T(8,128)S(1)}, u32[]{:S(2)}, u32[]{:S(2)}) %collective-permute-start) | collective-permute-done | bytes 32800 | tf_op jit(solution)/shard_map/ppermute | solution.py:240
  73.4 0.7 copy.22
  (36 shorter events, 1.0 us)
Async XLA Ops:
  0.6 16.9 %copy-start.2 = (s32[1,2]{1,0:T(1,128)S(1)}, s32[1,2]{1,0:T(1,128)}, u32[]{:S(2)}) copy-start(s32[1,2]{1,0:T(1,128)} %offset_ref.1) | copy-start | bytes 28
  0.6 22.3 %copy-start.8 = (s32[1,1,32]{2,1,0:T(1,128)S(1)}, s32[1,1,32]{2,1,0:T(1,128)}, u32[]{:S(2)}) copy-start(s32[1,1,32]{2,1,0:T(1,128)} %param.20) | copy-start | bytes 388
  0.7 22.5 %copy-start.9 = (s32[1,1,2]{2,1,0:T(1,128)S(1)}, s32[1,1,2]{2,1,0:T(1,128)}, u32[]{:S(2)}) copy-start(s32[1,1,2]{2,1,0:T(1,128)} %param.19) | copy-start | bytes 28
  0.7 31.2 %copy-start.5 = (s32[1,1,32]{2,1,0:T(1,128)S(1)}, s32[1,1,32]{2,1,0:T(1,128)}, u32[]{:S(2)}) copy-start(s32[1,1,32]{2,1,0:T(1,128)} %param.21) | copy-start | bytes 388
  0.7 31.2 %copy-start.4 = (bf16[1,1,2,128,512]{4,3,2,1,0:T(8,128)(2,1)S(1)}, bf16[1,1,2,128,512]{4,3,2,1,0:T(8,128)(2,1)}, u32[]{:S(2)}) copy-start(bf16[1,1,2,128,512]{4,3,2,1,0:T(8,128)(2,1)} %param.13) | copy-start | bytes 786436
  0.7 31.2 %copy-start.3 = (f32[1,1,2,128,512]{4,3,2,1,0:T(8,128)S(1)}, f32[1,1,2,128,512]{4,3,2,1,0:T(8,128)}, u32[]{:S(2)}) copy-start(f32[1,1,2,128,512]{4,3,2,1,0:T(8,128)} %param.12) | copy-start | bytes 1572868
  2.4 15.1 %all-to-all-start = ((bf16[32,16,128]{2,1,0:T(8,128)(2,1)}), bf16[32,16,128]{2,1,0:T(8,128)(2,1)S(1)}, u32[]{:S(2)}, u32[]{:S(2)}) async-start(bf16[32,16,128]{2,1,0:T(8,128)(2,1)} %bitcast.4), calls=%async_computation | async-start | bytes 262144 | tf_op jit(solution)/shard_map/all_to_all | solution.py:169
  18.8 13.0 %all-to-all-start.1 = ((bf16[32,32,128]{2,1,0:T(8,128)(2,1)}), bf16[32,32,128]{2,1,0:T(8,128)(2,1)S(1)}, u32[]{:S(2)}, u32[]{:S(2)}) async-start(bf16[32,32,128]{2,1,0:T(8,128)(2,1)} %shard_map.131), calls=%async_computation.1 | async-start | bytes 524288 | tf_op jit(solution)/shard_map/all_to_all | solution.py:169
  24.4 0.8 %copy-start.6 = (bf16[1024,256]{1,0:T(8,128)(2,1)}, bf16[1024,256]{1,0:T(8,128)(2,1)S(1)}, u32[]{:S(2)}) copy-start(bf16[1024,256]{1,0:T(8,128)(2,1)S(1)} %get-tuple-element.7.band_ref) | copy-start | bytes 1572868
  31.8 1.0 %copy-start.7 = (bf16[1024,256]{1,0:T(8,128)(2,1)S(1)}, bf16[1024,256]{1,0:T(8,128)(2,1)}, u32[]{:S(2)}) copy-start(bf16[1024,256]{1,0:T(8,128)(2,1)} %copy-done.6) | copy-start | bytes 1572868
  61.2 12.1 %copy-start = (f32[1,1,3,4096]{3,1,2,0:T(1,128)S(1)}, f32[1,1,3,4096]{3,1,2,0:T(1,128)}, u32[]{:S(2)}) copy-start(f32[1,1,3,4096]{3,1,2,0:T(1,128)} %param.22) | copy-start | bytes 147460
  61.2 12.1 %copy-start.1 = (f32[1,1,3,4096]{3,1,2,0:T(1,128)S(1)}, f32[1,1,3,4096]{3,1,2,0:T(1,128)}, u32[]{:S(2)}) copy-start(f32[1,1,3,4096]{3,1,2,0:T(1,128)} %param.23) | copy-start | bytes 147460
  62.1 6.1 %collective-permute-start.1 = (f32[64,128]{1,0:T(8,128)S(1)}, f32[64,128]{1,0:T(8,128)S(1)}, u32[]{:S(2)}, u32[]{:S(2)}) collective-permute-start(f32[64,128]{1,0:T(8,128)S(1)} %get-tuple-element.18), channel_id=1, source_target_pairs={{32,0},{64,32},{96,64},{128,96},{160,128},{192,160},{224,192},{256... | collective-permute-start | bytes 98312 | tf_op jit(solution)/shard_map/ppermute | solution.py:241
  66.3 7.0 %collective-permute-start = (f32[64,128]{1,0:T(8,128)S(1)}, f32[64,128]{1,0:T(8,128)S(1)}, u32[]{:S(2)}, u32[]{:S(2)}) collective-permute-start(f32[64,128]{1,0:T(8,128)S(1)} %get-tuple-element.19), channel_id=1, source_target_pairs={{0,32},{32,64},{64,96},{96,128},{128,160},{160,192},{192,224},{224... | collective-permute-start | bytes 98312 | tf_op jit(solution)/shard_map/ppermute | solution.py:240

commit v2 on v1

v2 whole, which is shorter than its diff:
```python
import jax
import jax.numpy as jnp
from jax import lax
from jax.experimental.layout import Layout, with_layout_constraint
from jax.experimental import pallas as pl
from jax.experimental.pallas import tpu as pltpu
from jax.sharding import PartitionSpec as P

TILES = 32
VISITS = 2
H = 128
W = 512
BS = 64
NB = 8
TAPS = 21
HALF = 10
LANE = 128
CB = W // LANE
NBLK = 32
BPV = NBLK // VISITS
KERNELS = 20
PATCHES = 3
f32 = jnp.float32
bf16 = jnp.bfloat16
VMEM = pl.BlockSpec(memory_space=pltpu.VMEM)
SMEM = pl.BlockSpec(memory_space=pltpu.SMEM)


def call(kernel, outs, in_specs, cost, scratch=(), out_specs=None):
    return pl.pallas_call(
        kernel,
        out_shape=outs,
        in_specs=in_specs,
        out_specs=out_specs or jax.tree.map(lambda _: VMEM, outs),
        scratch_shapes=list(scratch),
        compiler_params=pltpu.CompilerParams(vmem_limit_bytes=24 * 2**20),
        cost_estimate=pl.CostEstimate(flops=cost[0], bytes_accessed=cost[1], transcendentals=0),
    )


def toeplitz(row, width):
    return pltpu.roll(jnp.broadcast_to(row, (LANE, width)), 0, 1, stride=1, stride_axis=0)


def prep_kernel(
    index_ref, owner_ref, slot_ref, count_ref, filters_ref, coeff_ref,
    band_ref, both_ref, from_ref, slots_ref, seen_ref, taps_ref, weight_ref, eff_ref,
):
    for p in range(2 * TILES):
        from_ref[p] = NBLK
        slots_ref[p] = 0
    for o in range(TILES):
        seen_ref[o] = 0
    for r in range(NBLK):
        owner = owner_ref[r]
        repeat = seen_ref[owner]
        seen_ref[owner] = repeat + 1
        place = 2 * owner + repeat
        counted = r % BPV < count_ref[r // BPV]
        from_ref[place] = jnp.where(counted, r, NBLK)
        slots_ref[place] = slot_ref[r]

    taps_ref[...] = jnp.zeros_like(taps_ref)
    taps_ref[:, pl.ds(0, TAPS)] = filters_ref[...].astype(f32)
    taps_ref[...] = pltpu.roll(taps_ref[...], 2 * LANE - HALF, 1)
    weight_ref[...] = jnp.zeros_like(weight_ref)
    for v in range(VISITS):
        weight_ref[pl.ds(3 * v, 3), pl.ds(0, KERNELS)] = coeff_ref[v]
    eff_ref[...] = jnp.zeros_like(eff_ref)
    for k in range(KERNELS):
        r, c = index_ref[0, k], index_ref[1, k]
        taps = jnp.broadcast_to(taps_ref[pl.ds(c, 1), :], (8, 2 * LANE))
        weight = jnp.broadcast_to(weight_ref[:, k : k + 1], (8, 2 * LANE))
        eff_ref[r] = eff_ref[r] + weight * taps

    for j in range(NB):
        band_ref[pl.ds(j * LANE, LANE), :] = toeplitz(taps_ref[j : j + 1, :], 2 * LANE).astype(bf16)
    row = lax.broadcasted_iota(jnp.int32, (H, H), 0)
    col = lax.broadcasted_iota(jnp.int32, (H, H), 1)
    inside = jnp.abs(row - col) <= HALF
    down = (2.0 * row.astype(f32) + 1.0 - H) / H
    for v in range(VISITS):
        for r in range(NB):
            rows = eff_ref[r]
            rows = rows[:, :LANE] + rows[:, LANE:]
            parts = [toeplitz(rows[3 * v + t : 3 * v + t + 1], H) for t in range(3)]
            for m, value in enumerate((parts[0] + down * parts[2], parts[1])):
                value = jnp.where(inside, value, 0.0)
                high = value.astype(bf16)
                both_ref[v, pl.ds(m * H, H), pl.ds(r * H, H)] = high
                both_ref[v, pl.ds((2 + m) * H, H), pl.ds(r * H, H)] = (value - high.astype(f32)).astype(bf16)


def roll_kernel(offset_ref, held_ref, out_ref):
    for v in range(VISITS):
        offset = offset_ref[0, v]
        for i in range(TILES):
            out_ref[i, pl.ds(v * 16, 16), :] = held_ref[(offset + i) & (TILES - 1)]


def spread(plane, blocks_ref, v):
    left = lax.broadcasted_iota(jnp.int32, (BS, LANE), 1) < BS
    for by in range(H // BS):
        for pair in range(CB):
            here = plane[by * BS : (by + 1) * BS, pair * LANE : (pair + 1) * LANE]
            there = pltpu.roll(here, BS, 1)
            r = v * BPV + by * (W // BS) + pair * 2
            blocks_ref[r] = jnp.where(left, here, there).astype(bf16)
            blocks_ref[r + 1] = jnp.where(left, there, here).astype(bf16)


def pack(from_ref, blocks_ref, payload_ref, top):
    left = lax.broadcasted_iota(jnp.int32, (BS, LANE), 1) < BS
    for o in range(TILES):
        payload_ref[o, pl.ds(top, BS), :] = jnp.where(
            left, blocks_ref[from_ref[2 * o]], blocks_ref[from_ref[2 * o + 1]]
        )


def main_kernel(
    from_ref, slots_ref, arrived_ref, band_ref, both_ref, science_ref, inverse_ref,
    difference_ref, payload_ref, window_ref, filtered_ref, blocks_ref, weights_ref,
):
    lane = lax.broadcasted_iota(jnp.int32, (H, LANE), 1)
    across = (2.0 * lax.broadcasted_iota(jnp.int32, (H, W), 1).astype(f32) + 1.0 - W) / W
    zero = jnp.zeros((H, LANE), bf16)
    blocks_ref[NBLK] = jnp.zeros((BS, LANE), bf16)
    weights_ref[NBLK] = jnp.zeros((BS, LANE), bf16)
    for v in range(VISITS):
        tiles = [
            jnp.concatenate(
                [arrived_ref[2 * rt + b // 2, pl.ds(v * 16 + b % 2 * 8, 8), :] for rt in range(H // 8)], axis=0
            )
            for b in range(CB)
        ]
        for b in range(CB):
            after = tiles[b + 1] if b + 1 < CB else zero
            before = tiles[b - 1] if b > 0 else zero
            rows = pl.ds((v * CB + b) * H, H)
            window_ref[rows, pl.ds(0, LANE)] = tiles[b]
            window_ref[rows, pl.ds(LANE, LANE)] = jnp.where(lane < BS, after, before)
    for jj in range(NB // 2):
        rows = lax.dot_general(
            window_ref[...],
            band_ref[pl.ds(jj * 2 * LANE, 2 * LANE), :],
            (((1,), (1,)), ((), ())),
            preferred_element_type=f32,
        ).astype(bf16)
        for v in range(VISITS):
            for b in range(CB):
                for j in range(2):
                    top = (v * CB + b) * H
                    filtered_ref[v, pl.ds((2 * jj + j) * H, H), pl.ds(b * LANE, LANE)] = rows[
                        top : top + H, j * LANE : (j + 1) * LANE
                    ]
    for v in range(VISITS):
        both = jnp.dot(both_ref[v], filtered_ref[v], preferred_element_type=f32)
        both = both[: 2 * H] + both[2 * H :]
        difference = science_ref[v] - (both[:H] + across * both[H:])
        difference_ref[v] = difference
        inverse = inverse_ref[v].astype(f32)
        spread(inverse, weights_ref, v)
        spread(inverse * difference, blocks_ref, v)
    pack(from_ref, blocks_ref, payload_ref, 0)
    pack(from_ref, weights_ref, payload_ref, BS)
    left = lax.broadcasted_iota(jnp.int32, (8, LANE), 1) < BS
    for o in range(TILES):
        slots = [jnp.full((8, LANE), slots_ref[2 * o + k], jnp.int32) for k in range(2)]
        payload_ref[o, pl.ds(2 * BS, 8), :] = jnp.where(left, slots[0], slots[1]).astype(f32).astype(bf16)


def sum_kernel(arrived_ref, total_ref):
    left = lax.broadcasted_iota(jnp.int32, (BS, LANE), 1) < BS
    sums = []
    for part in range(2):
        def body(j, acc):
            head = arrived_ref[j, pl.ds(2 * BS, 8), :].astype(f32)[:1]
            value = arrived_ref[j, pl.ds(part * BS, BS), :].astype(f32)
            return tuple(
                acc[s] + jnp.where(jnp.broadcast_to(head == s, (BS, LANE)), value, 0.0) for s in range(PATCHES)
            )

        acc = lax.fori_loop(0, TILES, body, tuple(jnp.zeros((BS, LANE), f32) for _ in range(PATCHES)), unroll=4)
        sums.append([a + pltpu.roll(a, BS, 1) for a in acc])
    for s in range(PATCHES):
        total_ref[s] = jnp.where(left, sums[0][s], sums[1][s])


def final_kernel(total_ref, low_ref, high_ref, sum_ref, weight_ref, out_ref, merged_ref):
    left = lax.broadcasted_iota(jnp.int32, (BS // 2, LANE), 1) < BS
    for s in range(PATCHES):
        merged = total_ref[s]
        if s == 0:
            merged = merged + low_ref[...]
        if s == PATCHES - 1:
            merged = merged + high_ref[...]
        merged_ref[...] = merged
        even = merged_ref[pl.ds(0, BS // 2, stride=2), :]
        odd = merged_ref[pl.ds(1, BS // 2, stride=2), :]
        value = jnp.where(left, even, pltpu.roll(odd, BS, 1))
        weight = jnp.where(left, pltpu.roll(even, BS, 1), odd)
        out_ref[s] = (sum_ref[s] + value) / (weight_ref[s] + weight)


def all_to_all(x):
    return lax.all_to_all(x, "tile", split_axis=0, concat_axis=0, tiled=True)


def shards(
    science,
    inverse_variance,
    template,
    filters,
    kernel_index,
    spatial_coeff,
    visit_offset,
    block_count,
    block_owner,
    block_slot,
    coadd_sum,
    coadd_weight,
):
    sds = jax.ShapeDtypeStruct
    tiles = template[0, 0].reshape(H // 8, 8, CB, LANE)
    tiles = with_layout_constraint(tiles, Layout(major_to_minor=(0, 2, 1, 3)))
    held = all_to_all(tiles.transpose(0, 2, 1, 3).reshape(TILES, 16, LANE))
    outgoing = call(
        roll_kernel, sds((TILES, VISITS * 16, LANE), bf16), [SMEM, VMEM], (0, 400_000)
    )(visit_offset, held)

    outgoing, index = lax.optimization_barrier((outgoing, kernel_index.T))
    band, both, origin, slots = call(
        prep_kernel,
        (
            sds((NB * LANE, 2 * LANE), bf16),
            sds((VISITS, 4 * H, NB * H), bf16),
            sds((2 * TILES,), jnp.int32),
            sds((2 * TILES,), jnp.int32),
        ),
        [SMEM, SMEM, SMEM, SMEM, VMEM, VMEM],
        (10_000_000, 3_000_000),
        [
            pltpu.SMEM((TILES,), jnp.int32),
            pltpu.VMEM((NB, 2 * LANE), f32),
            pltpu.VMEM((8, LANE), f32),
            pltpu.VMEM((NB, 8, 2 * LANE), f32),
        ],
        (VMEM, VMEM, SMEM, SMEM),
    )(index, block_owner[0, 0], block_slot[0, 0], block_count[0, 0], filters, spatial_coeff[0, 0])
    arrived = all_to_all(outgoing)

    blocks = pltpu.VMEM((NBLK + 1, BS, LANE), bf16)
    difference, payload = call(
        main_kernel,
        (sds((VISITS, H, W), f32), sds((TILES, 2 * BS + 8, LANE), bf16)),
        [SMEM, SMEM] + [VMEM] * 5,
        (2_000_000_000, 6_000_000),
        [
            pltpu.VMEM((VISITS * CB * H, 2 * LANE), bf16),
            pltpu.VMEM((VISITS, NB * H, W), bf16),
            blocks,
            blocks,
        ],
    )(origin, slots, arrived, band, both, science[0, 0], inverse_variance[0, 0])

    total = call(
        sum_kernel, sds((PATCHES, BS, LANE), f32), [VMEM], (5_000_000, 1_300_000)
    )(all_to_all(payload))

    count = lax.axis_size("sky")
    low = lax.ppermute(total[PATCHES - 1], "sky", [(i, i + 1) for i in range(count - 1)])
    high = lax.ppermute(total[0], "sky", [(i + 1, i) for i in range(count - 1)])
    result = call(
        final_kernel,
        sds((PATCHES, BS // 2, LANE), f32),
        [VMEM] * 5,
        (100_000, 300_000),
        [pltpu.VMEM((BS, LANE), f32)],
    )(
        total,
        low,
        high,
        coadd_sum[0, 0].reshape(PATCHES, BS // 2, LANE),
        coadd_weight[0, 0].reshape(PATCHES, BS // 2, LANE),
    )
    return (difference[None, None], result.reshape(1, 1, PATCHES, BS * BS))


def solution(mesh):
    return jax.shard_map(
        shards,
        mesh=mesh,
        in_specs=(
            P("sky", "tile", None, None, None),
            P("sky", "tile", None, None, None),
            P("sky", "tile", None, None),
            P(),
            P(),
            P("sky", "tile", None, None, None),
            P("sky", None),
            P("sky", "tile", None),
            P("sky", "tile", None),
            P("sky", "tile", None),
            P("sky", "tile", None, None),
            P("sky", "tile", None, None),
        ),
        out_specs=(P("sky", "tile", None, None, None), P("sky", "tile", None, None)),
        check_vma=False,
    )
```

time: 74.6 us -> 70.7 us (0.948)
  blocking collectives: 22.5 us -> 37.4 us
  starting transfers between devices: 17.5 us -> 9.92 us
  waiting for transfers between devices: 15.1 us -> 8.91 us
  local copies, waits for them, and re-layouts: 7.5 us -> 4.4 us
  other arithmetic: 1.53 us -> 0 us
    all_to_all x1 -> x2, blocking collectives: 22.5 us -> 37.4 us  [all_to_all(): return lax.all_to_all(x, 'tile', split_axis=0, concat_axis=0, tiled=True)]
    all_to_all x2 -> x1, starting transfers between devices: 11.4 us -> 3.87 us  [all_to_all(): return lax.all_to_all(x, 'tile', split_axis=0, concat_axis=0, tiled=True)]
    all_to_all x2 -> x1, waiting for transfers between devices: 9.97 us -> 3.83 us  [all_to_all(): return lax.all_to_all(x, 'tile', split_axis=0, concat_axis=0, tiled=True)]
    another operation x2 -> x0, local copies, waits for them, and re-layouts: 1.69 us -> none  [shards(): template[0, 0].reshape(H // 16, 16, CB, LANE).transpose(0, 2, 1, 3)]
    slice x3 -> x0, local copies, waits for them, and re-layouts: 1.51 us -> none  [centred(): return jnp.concatenate([rows[:, HALF:], gap, rows[:, :HALF]], axis=1)]
    convert_element_type x3 -> x0, other arithmetic: 0.83 us -> none  [the longest x1 0.68 us: shards(): taps = filters.astype(f32)]
    eq x1 -> x0, local copies, waits for them, and re-layouts: 0.76 us -> none  [shards(): row_pick = (kernel_index[:, 0, None] == ids[None, :]).astype(f32)]
    unnamed x22 -> x20, local copies, waits for them, and re-layouts: 3.21 us -> 3.71 us
  transfers between devices with their start and end apart: 4 -> 3, of which waited for: 3 -> 2; matrix products, arithmetic and copies ran while one was open for 6% -> 1% of each run, Pallas kernels for 1% -> 3%
where the time goes in v2:
time: 70.7 us; the launch traced here: 70.2 us
  blocking collectives  37.4 us (53%)
  starting transfers between devices  9.92 us (14%)
  Pallas kernels  8.91 us (13%)
  waiting for transfers between devices  8.91 us (13%)
  local copies, waits for them, and re-layouts  4.4 us (6%)
  between operations  0.73 us (1%)
    all_to_all x2, blocking collectives, all_to_all(): return lax.all_to_all(x, 'tile', split_axis=0, concat_axis=0, tiled=True)  37.4 us
    ppermute x1, waiting for transfers between devices, shards(): lax.ppermute(total[PATCHES - 1], 'sky', [(i, i + 1) for i in range(count...  5.08 us
    ppermute x1, starting transfers between devices, shards(): high = lax.ppermute(total[0], 'sky', [(i + 1, i) for i in range(count - 1)])  4.13 us
    all_to_all x1, starting transfers between devices, all_to_all(): return lax.all_to_all(x, 'tile', split_axis=0, concat_axis=0, tiled=True)  3.87 us
    all_to_all x1, waiting for transfers between devices, all_to_all(): return lax.all_to_all(x, 'tile', split_axis=0, concat_axis=0, tiled=True)  3.83 us
    unnamed x20, local copies, waits for them, and re-layouts  3.71 us
    pallas_call x1, Pallas kernels, shards(): call(main_kernel, (sds((VISITS, H, W), f32), sds((TILES, 2 * BS + 8, LANE...  3.62 us
    pallas_call x1, Pallas kernels, shards(): call(prep_kernel, (sds((NB * LANE, 2 * LANE), bf16), sds((VISITS, 4 * H,...  2.37 us
  transfers between devices with their start and end apart: 3, of which 2 were waited for; matrix products, arithmetic and copies ran while one was open for 1% of the time, Pallas kernels for 3%

profile of v2, /device:TPU:384, one launch (start us, length us, event | category | flops | bytes accessed | tf_op | source)
XLA Modules:
  0.0 70.2 jit_solution(8867410892871594129)
XLA Ops:
  0.6 0.0 copy-start.6
  0.6 0.0 copy-start.7
  0.7 15.3 %all_to_all.15.held_ref = bf16[32,16,128]{2,1,0:T(8,128)(2,1)S(1)} all-to-all(bf16[32,16,128]{2,1,0:T(8,128)(2,1)} %bitcast.28), channel_id=1, replica_groups=mesh['sky'=16,'tile'=32] {'tile'}, dimensions={0} | all-to-all | bytes 262144 | tf_op jit(solution)/shard_map/all_to_all | solution.py:206
  15.9 0.7 copy-done.2
  16.6 1.3 %shard_map.131 = bf16[32,32,128]{2,1,0:T(8,128)(2,1)} custom-call(s32[1,2]{1,0:T(1,128)S(1)} %copy-done.2, bf16[32,16,128]{2,1,0:T(8,128)(2,1)S(1)} %all_to_all.15.held_ref), custom_call_target="tpu_custom_call" | custom-call | bytes 400000 | tf_op jit(solution)/shard_map/pallas_call | solution.py:227
  17.9 3.9 %all-to-all-start.1 = ((bf16[32,32,128]{2,1,0:T(8,128)(2,1)}), bf16[32,32,128]{2,1,0:T(8,128)(2,1)S(1)}, u32[]{:S(2)}, u32[]{:S(2)}) async-start(bf16[32,32,128]{2,1,0:T(8,128)(2,1)} %shard_map.131), calls=%async_computation.1 | async-start | bytes 524288 | tf_op jit(solution)/shard_map/all_to_all | solution.py:206
  21.8 0.7 copy.16.coeff_ref
  22.5 0.0 copy-done.6
  22.5 0.7 copy-done.5
  23.1 0.7 copy-done.8
  23.8 0.7 copy-done.9
  24.5 2.4 %shard_map.132 = (bf16[1024,256]{1,0:T(8,128)(2,1)S(1)}, bf16[2,512,1024]{2,1,0:T(8,128)(2,1)S(1)}, s32[64]{0:T(128)S(1)}, s32[64]{0:T(128)S(1)}) custom-call(s32[2,20]{1,0:T(2,128)S(1)} %bitcast.24, s32[32]{0:T(128)S(1)} %bitcast.25, s32[32]{0:T(128)S(1)} %bitcast.26, s32[2]{0:T(128)S(1)} %bitcast.27, bf16[8,21]{1,0:T(8,128)(2,1)S(1)} %copy-done.5, ...), custom_call_target="tpu_custom_call" | custom-call | flops 10000000 | bytes 3000000 | tf_op jit(solution)/shard_map/pallas_call | solution.py:232
  26.8 3.8 %all-to-all-done.1.arrived_ref = bf16[32,32,128]{2,1,0:T(8,128)(2,1)S(1)} async-done(((bf16[32,32,128]{2,1,0:T(8,128)(2,1)}), bf16[32,32,128]{2,1,0:T(8,128)(2,1)S(1)}, u32[]{:S(2)}, u32[]{:S(2)}) %all-to-all-start.1) | async-done | bytes 262176 | tf_op jit(solution)/shard_map/all_to_all | solution.py:206
  30.7 0.0 copy-done.4
  30.7 1.0 %copy-done.3 = f32[1,1,2,128,512]{4,3,2,1,0:T(8,128)S(1)} copy-done((f32[1,1,2,128,512]{4,3,2,1,0:T(8,128)S(1)}, f32[1,1,2,128,512]{4,3,2,1,0:T(8,128)}, u32[]{:S(2)}) %copy-start.3) | copy-done | bytes 524312
  31.7 3.6 %shard_map.133 = (f32[2,128,512]{2,1,0:T(8,128)}, bf16[32,136,128]{2,1,0:T(8,128)(2,1)S(1)}) custom-call(s32[64]{0:T(128)S(1)} %get-tuple-element.11.from_ref, s32[64]{0:T(128)S(1)} %get-tuple-element.12.slots_ref, bf16[32,32,128]{2,1,0:T(8,128)(2,1)S(1)} %all-to-all-done.1.arrived_ref, bf16[1024,256]{1,0:T(8,128)(2,1)S(1)} %get-tuple-element.14.band_ref, ...), custom_call_target="tpu_custom_call" | custom-call | flops 2000000000 | bytes 6000000 | tf_op jit(solution)/shard_map/pallas_call | solution.py:253
  35.3 22.1 %all_to_all.16.arrived_ref = bf16[32,136,128]{2,1,0:T(8,128)(2,1)S(1)} all-to-all(bf16[32,136,128]{2,1,0:T(8,128)(2,1)S(1)} %get-tuple-element.17), channel_id=1, replica_groups=mesh['sky'=16,'tile'=32] {'tile'}, dimensions={0} | all-to-all | bytes 2228224 | tf_op jit(solution)/shard_map/all_to_all | solution.py:206
  57.4 0.9 %shard_map.134.total_ref = f32[3,64,128]{2,1,0:T(8,128)S(1)} custom-call(bf16[32,136,128]{2,1,0:T(8,128)(2,1)S(1)} %all_to_all.16.arrived_ref), custom_call_target="tpu_custom_call" | custom-call | flops 5000000 | bytes 1300000 | tf_op jit(solution)/shard_map/pallas_call | solution.py:266
  58.3 4.1 %collective-permute-start.1 = (f32[64,128]{1,0:T(8,128)S(1)}, f32[64,128]{1,0:T(8,128)S(1)}, u32[]{:S(2)}, u32[]{:S(2)}) collective-permute-start(f32[64,128]{1,0:T(8,128)S(1)} %get-tuple-element.22), channel_id=1, source_target_pairs={{32,0},{64,32},{96,64},{128,96},{160,128},{192,160},{224,192},{256... | collective-permute-start | bytes 98312 | tf_op jit(solution)/shard_map/ppermute | solution.py:272
  62.5 1.9 %collective-permute-start = (f32[64,128]{1,0:T(8,128)S(1)}, f32[64,128]{1,0:T(8,128)S(1)}, u32[]{:S(2)}, u32[]{:S(2)}) collective-permute-start(f32[64,128]{1,0:T(8,128)S(1)} %get-tuple-element.23), channel_id=1, source_target_pairs={{0,32},{32,64},{64,96},{96,128},{128,160},{160,192},{192,224},{224... | collective-permute-start | bytes 98312 | tf_op jit(solution)/shard_map/ppermute | solution.py:271
  64.4 0.0 collective-permute-done.1.high_ref
  64.4 5.1 %collective-permute-done.low_ref = f32[64,128]{1,0:T(8,128)S(1)} collective-permute-done((f32[64,128]{1,0:T(8,128)S(1)}, f32[64,128]{1,0:T(8,128)S(1)}, u32[]{:S(2)}, u32[]{:S(2)}) %collective-permute-start) | collective-permute-done | bytes 32800 | tf_op jit(solution)/shard_map/ppermute | solution.py:271
  69.5 0.0 copy-done.1
  69.5 0.7 %shard_map.135 = f32[3,32,128]{2,1,0:T(8,128)} custom-call(f32[3,64,128]{2,1,0:T(8,128)S(1)} %shard_map.134.total_ref, f32[64,128]{1,0:T(8,128)S(1)} %collective-permute-done.low_ref, f32[64,128]{1,0:T(8,128)S(1)} %collective-permute-done.1.high_ref, f32[3,32,128]{2,1,0:T(8,128)S(1)} %bitcast.20, f32[3,32,128]{2,1,0:T(8,128)S(1)} %bitcast.21), custom_call_target="tpu_custom_call" | custom-call | flops 100000 | bytes 300000 | tf_op jit(solution)/shard_map/pallas_call | solution.py:273
  (11 shorter events, 0.0 us)
Async XLA Ops:
  0.6 21.8 %copy-start.6 = (s32[20,2]{0,1:T(2,128)S(1)}, s32[20,2]{0,1:T(2,128)}, u32[]{:S(2)}) copy-start(s32[20,2]{0,1:T(2,128)} %param.16) | copy-start | bytes 484
  0.6 21.8 %copy-start.7 = (s32[1,1,32]{2,1,0:T(1,128)S(1)}, s32[1,1,32]{2,1,0:T(1,128)}, u32[]{:S(2)}) copy-start(s32[1,1,32]{2,1,0:T(1,128)} %param.20) | copy-start | bytes 388
  0.7 30.0 %copy-start.4 = (bf16[1,1,2,128,512]{4,3,2,1,0:T(8,128)(2,1)S(1)}, bf16[1,1,2,128,512]{4,3,2,1,0:T(8,128)(2,1)}, u32[]{:S(2)}) copy-start(bf16[1,1,2,128,512]{4,3,2,1,0:T(8,128)(2,1)} %param.13) | copy-start | bytes 786436
  15.9 0.7 copy-start.2
  17.9 12.8 %all-to-all-start.1 = ((bf16[32,32,128]{2,1,0:T(8,128)(2,1)}), bf16[32,32,128]{2,1,0:T(8,128)(2,1)S(1)}, u32[]{:S(2)}, u32[]{:S(2)}) async-start(bf16[32,32,128]{2,1,0:T(8,128)(2,1)} %shard_map.131), calls=%async_computation.1 | async-start | bytes 524288 | tf_op jit(solution)/shard_map/all_to_all | solution.py:206
  22.5 0.7 copy-start.5
  23.1 0.7 copy-start.8
  23.8 0.7 copy-start.9
  30.7 1.0 %copy-start.3 = (f32[1,1,2,128,512]{4,3,2,1,0:T(8,128)S(1)}, f32[1,1,2,128,512]{4,3,2,1,0:T(8,128)}, u32[]{:S(2)}) copy-start(f32[1,1,2,128,512]{4,3,2,1,0:T(8,128)} %param.12) | copy-start | bytes 1572868
  57.4 12.1 %copy-start = (f32[1,1,3,4096]{3,1,2,0:T(1,128)S(1)}, f32[1,1,3,4096]{3,1,2,0:T(1,128)}, u32[]{:S(2)}) copy-start(f32[1,1,3,4096]{3,1,2,0:T(1,128)} %param.22) | copy-start | bytes 147460
  57.4 12.1 %copy-start.1 = (f32[1,1,3,4096]{3,1,2,0:T(1,128)S(1)}, f32[1,1,3,4096]{3,1,2,0:T(1,128)}, u32[]{:S(2)}) copy-start(f32[1,1,3,4096]{3,1,2,0:T(1,128)} %param.23) | copy-start | bytes 147460
  58.3 6.1 %collective-permute-start.1 = (f32[64,128]{1,0:T(8,128)S(1)}, f32[64,128]{1,0:T(8,128)S(1)}, u32[]{:S(2)}, u32[]{:S(2)}) collective-permute-start(f32[64,128]{1,0:T(8,128)S(1)} %get-tuple-element.22), channel_id=1, source_target_pairs={{32,0},{64,32},{96,64},{128,96},{160,128},{192,160},{224,192},{256... | collective-permute-start | bytes 98312 | tf_op jit(solution)/shard_map/ppermute | solution.py:272
  62.5 7.0 %collective-permute-start = (f32[64,128]{1,0:T(8,128)S(1)}, f32[64,128]{1,0:T(8,128)S(1)}, u32[]{:S(2)}, u32[]{:S(2)}) collective-permute-start(f32[64,128]{1,0:T(8,128)S(1)} %get-tuple-element.23), channel_id=1, source_target_pairs={{0,32},{32,64},{64,96},{96,128},{128,160},{160,192},{192,224},{224... | collective-permute-start | bytes 98312 | tf_op jit(solution)/shard_map/ppermute | solution.py:271

commit v3 on v2

--- a/solution.py
+++ b/solution.py
@@ -23,6 +23,7 @@
 f32 = jnp.float32
 bf16 = jnp.bfloat16
 VMEM = pl.BlockSpec(memory_space=pltpu.VMEM)
+ANY = pl.BlockSpec(memory_space=pl.ANY)
 SMEM = pl.BlockSpec(memory_space=pltpu.SMEM)
 
 
@@ -42,60 +43,112 @@
     return pltpu.roll(jnp.broadcast_to(row, (LANE, width)), 0, 1, stride=1, stride_axis=0)
 
 
-def prep_kernel(
-    index_ref, owner_ref, slot_ref, count_ref, filters_ref, coeff_ref,
-    band_ref, both_ref, from_ref, slots_ref, seen_ref, taps_ref, weight_ref, eff_ref,
-):
-    for p in range(2 * TILES):
-        from_ref[p] = NBLK
-        slots_ref[p] = 0
-    for o in range(TILES):
-        seen_ref[o] = 0
-    for r in range(NBLK):
-        owner = owner_ref[r]
-        repeat = seen_ref[owner]
-        seen_ref[owner] = repeat + 1
-        place = 2 * owner + repeat
-        counted = r % BPV < count_ref[r // BPV]
-        from_ref[place] = jnp.where(counted, r, NBLK)
-        slots_ref[place] = slot_ref[r]
-
+def effective_taps(index_ref, filters_ref, coeff_ref, taps_ref, weight_ref):
     taps_ref[...] = jnp.zeros_like(taps_ref)
-    taps_ref[:, pl.ds(0, TAPS)] = filters_ref[...].astype(f32)
-    taps_ref[...] = pltpu.roll(taps_ref[...], 2 * LANE - HALF, 1)
+    taps_ref[pl.ds(0, NB), pl.ds(0, TAPS)] = filters_ref[...].astype(f32)
+    taps_ref[pl.ds(0, NB), :] = pltpu.roll(taps_ref[pl.ds(0, NB), :], 2 * LANE - HALF, 1)
     weight_ref[...] = jnp.zeros_like(weight_ref)
     for v in range(VISITS):
-        weight_ref[pl.ds(3 * v, 3), pl.ds(0, KERNELS)] = coeff_ref[v]
-    eff_ref[...] = jnp.zeros_like(eff_ref)
-    for k in range(KERNELS):
-        r, c = index_ref[0, k], index_ref[1, k]
-        taps = jnp.broadcast_to(taps_ref[pl.ds(c, 1), :], (8, 2 * LANE))
-        weight = jnp.broadcast_to(weight_ref[:, k : k + 1], (8, 2 * LANE))
-        eff_ref[r] = eff_ref[r] + weight * taps
-
-    for j in range(NB):
-        band_ref[pl.ds(j * LANE, LANE), :] = toeplitz(taps_ref[j : j + 1, :], 2 * LANE).astype(bf16)
+        weight_ref[pl.ds(3 * v, 3), pl.ds(0, KERNELS)] = coeff_ref[:, v, :]
+    weight_ref[pl.ds(8, 2), pl.ds(0, KERNELS)] = index_ref[...].astype(f32)
+    weight = weight_ref[pl.ds(0, 8), :]
+    rows = jnp.broadcast_to(weight_ref[8:9, :], (8, LANE))
+    columns = jnp.broadcast_to(weight_ref[9:10, :], (LANE, LANE))
+    picked = jnp.concatenate([jnp.where(rows == r, weight, 0.0) for r in range(NB)], axis=0)
+    one = (lax.broadcasted_iota(jnp.int32, (LANE, LANE), 0).astype(f32) == columns).astype(f32)
+    by_column = lax.dot_general(
+        picked, one, (((1,), (1,)), ((), ())), precision=lax.Precision.HIGHEST, preferred_element_type=f32
+    )
+    taps = taps_ref[:, pl.ds(0, LANE)] + taps_ref[:, pl.ds(LANE, LANE)]
+    return jnp.dot(by_column, taps, precision=lax.Precision.HIGHEST, preferred_element_type=f32)
+
+
+def column_bands(eff_ref, both_ref):
     row = lax.broadcasted_iota(jnp.int32, (H, H), 0)
-    col = lax.broadcasted_iota(jnp.int32, (H, H), 1)
-    inside = jnp.abs(row - col) <= HALF
+    inside = jnp.abs(row - lax.broadcasted_iota(jnp.int32, (H, H), 1)) <= HALF
     down = (2.0 * row.astype(f32) + 1.0 - H) / H
+
+    def body(n, carry):
+        v, r = n // NB, n % NB
+        cols = pl.ds(pl.multiple_of(r * H, H), H)
+        wide = [jnp.broadcast_to(eff_ref[pl.ds(8 * r + 3 * v + t, 1), :], (H, H)) for t in range(3)]
+        for m, value in enumerate((wide[0] + down * wide[2], wide[1])):
+            value = jnp.where(inside, pltpu.roll(value, 0, 1, stride=1, stride_axis=0), 0.0)
+            high = value.astype(bf16)
+            both_ref[v, pl.ds(m * H, H), cols] = high
+            both_ref[v, pl.ds((2 + m) * H, H), cols] = (value - high.astype(f32)).astype(bf16)
+        return carry
+
+    lax.fori_loop(0, VISITS * NB, body, 0)
+
+
+def pack_weights(from_ref, slots_ref, inverse_ref, payload_ref, blocks_ref):
+    left = lax.broadcasted_iota(jnp.int32, (BS, LANE), 1) < BS
+    blocks_ref[NBLK] = jnp.zeros((BS, LANE), bf16)
+
+    def spread_pair(n, carry):
+        v, by, pair = n // 8, n // CB % 2, n % CB
+        here = inverse_ref[
+            v, pl.ds(pl.multiple_of(by * BS, BS), BS), pl.ds(pl.multiple_of(pair * LANE, LANE), LANE)
+        ].astype(f32)
+        there = pltpu.roll(here, BS, 1)
+        blocks_ref[2 * n] = jnp.where(left, here, there).astype(bf16)
+        blocks_ref[2 * n + 1] = jnp.where(left, there, here).astype(bf16)
+        return carry
+
+    lax.fori_loop(0, NBLK // 2, spread_pair, 0)
+
+    def place(o, carry):
+        payload_ref[o, pl.ds(0, BS), :] = jnp.where(
+            left, blocks_ref[from_ref[2 * o]], blocks_ref[from_ref[2 * o + 1]]
+        )
+        slots = [jnp.full((8, LANE), slots_ref[2 * o + k], jnp.int32) for k in range(2)]
+        payload_ref[o, pl.ds(BS, 8), :] = jnp.where(left[:8], slots[0], slots[1]).astype(f32).astype(bf16)
+        return carry
+
+    lax.fori_loop(0, TILES, place, 0, unroll=2)
+
+
+def prep_kernel(
+    owner_ref, slot_ref, count_ref, index_ref, filters_ref, coeff_ref,
+    band_ref, eff_ref, from_ref, slots_ref, seen_ref, taps_ref, weight_ref,
+):
+    def clear(o, carry):
+        from_ref[2 * o] = NBLK
+        from_ref[2 * o + 1] = NBLK
+        slots_ref[2 * o] = 0
+        slots_ref[2 * o + 1] = 0
+        seen_ref[o] = 0
+        return carry
+
+    lax.fori_loop(0, TILES, clear, 0, unroll=4)
+    eff_ref[...] = effective_taps(index_ref, filters_ref, coeff_ref, taps_ref, weight_ref)
     for v in range(VISITS):
-        for r in range(NB):
-            rows = eff_ref[r]
-            rows = rows[:, :LANE] + rows[:, LANE:]
-            parts = [toeplitz(rows[3 * v + t : 3 * v + t + 1], H) for t in range(3)]
-            for m, value in enumerate((parts[0] + down * parts[2], parts[1])):
-                value = jnp.where(inside, value, 0.0)
-                high = value.astype(bf16)
-                both_ref[v, pl.ds(m * H, H), pl.ds(r * H, H)] = high
-                both_ref[v, pl.ds((2 + m) * H, H), pl.ds(r * H, H)] = (value - high.astype(f32)).astype(bf16)
-
-
-def roll_kernel(offset_ref, held_ref, out_ref):
-    for v in range(VISITS):
-        offset = offset_ref[0, v]
-        for i in range(TILES):
-            out_ref[i, pl.ds(v * 16, 16), :] = held_ref[(offset + i) & (TILES - 1)]
+        count = count_ref[v]
+
+        def put(i, carry, v=v, count=count):
+            r = v * BPV + i
+            owner = owner_ref[r]
+            repeat = seen_ref[owner]
+            seen_ref[owner] = repeat + 1
+            place = 2 * owner + repeat
+            from_ref[place] = jnp.where(i < count, r, NBLK)
+            slots_ref[place] = slot_ref[r]
+            return carry
+
+        lax.fori_loop(0, BPV, put, 0, unroll=2)
+
+    def band(j, carry):
+        rows = pl.ds(pl.multiple_of(j * LANE, LANE), LANE)
+        band_ref[rows, :] = toeplitz(taps_ref[pl.ds(j, 1), :], 2 * LANE).astype(bf16)
+        return carry
+
+    lax.fori_loop(0, NB, band, 0, unroll=2)
+
+
+def second_prep_kernel(from_ref, slots_ref, eff_ref, inverse_ref, both_ref, payload_ref, blocks_ref):
+    column_bands(eff_ref, both_ref)
+    pack_weights(from_ref, slots_ref, inverse_ref, payload_ref, blocks_ref)
 
 
 def spread(plane, blocks_ref, v):
@@ -109,30 +162,27 @@
             blocks_ref[r + 1] = jnp.where(left, there, here).astype(bf16)
 
 
-def pack(from_ref, blocks_ref, payload_ref, top):
-    left = lax.broadcasted_iota(jnp.int32, (BS, LANE), 1) < BS
-    for o in range(TILES):
-        payload_ref[o, pl.ds(top, BS), :] = jnp.where(
-            left, blocks_ref[from_ref[2 * o]], blocks_ref[from_ref[2 * o + 1]]
-        )
-
-
 def main_kernel(
-    from_ref, slots_ref, arrived_ref, band_ref, both_ref, science_ref, inverse_ref,
-    difference_ref, payload_ref, window_ref, filtered_ref, blocks_ref, weights_ref,
+    from_ref, tile0_ref, tile1_ref, band_ref, both_ref, weights_hbm, science_hbm, inverse_hbm,
+    difference_hbm, payload_hbm, window_ref, filtered_ref, blocks_ref,
+    science_ref, inverse_ref, difference_ref, payload_ref, sems,
 ):
+    def load(n, source, target):
+        copy = pltpu.make_async_copy(source, target, sems.at[n])
+        copy.start()
+        return copy
+
+    loads = [
+        load(0, inverse_hbm, inverse_ref),
+        load(2, science_hbm, science_ref),
+        load(3, weights_hbm, payload_hbm.at[:, pl.ds(BS, BS + 8), :]),
+    ]
     lane = lax.broadcasted_iota(jnp.int32, (H, LANE), 1)
     across = (2.0 * lax.broadcasted_iota(jnp.int32, (H, W), 1).astype(f32) + 1.0 - W) / W
     zero = jnp.zeros((H, LANE), bf16)
     blocks_ref[NBLK] = jnp.zeros((BS, LANE), bf16)
-    weights_ref[NBLK] = jnp.zeros((BS, LANE), bf16)
     for v in range(VISITS):
-        tiles = [
-            jnp.concatenate(
-                [arrived_ref[2 * rt + b // 2, pl.ds(v * 16 + b % 2 * 8, 8), :] for rt in range(H // 8)], axis=0
-            )
-            for b in range(CB)
-        ]
+        tiles = [(tile0_ref, tile1_ref)[v][:, b * LANE : (b + 1) * LANE] for b in range(CB)]
         for b in range(CB):
             after = tiles[b + 1] if b + 1 < CB else zero
             before = tiles[b - 1] if b > 0 else zero
@@ -153,20 +203,26 @@
                     filtered_ref[v, pl.ds((2 * jj + j) * H, H), pl.ds(b * LANE, LANE)] = rows[
                         top : top + H, j * LANE : (j + 1) * LANE
                     ]
+    for copy in loads:
+        copy.wait()
+    stores = []
     for v in range(VISITS):
         both = jnp.dot(both_ref[v], filtered_ref[v], preferred_element_type=f32)
         both = both[: 2 * H] + both[2 * H :]
         difference = science_ref[v] - (both[:H] + across * both[H:])
         difference_ref[v] = difference
+        stores.append(load(4 + v, difference_ref.at[v], difference_hbm.at[v]))
         inverse = inverse_ref[v].astype(f32)
-        spread(inverse, weights_ref, v)
         spread(inverse * difference, blocks_ref, v)
-    pack(from_ref, blocks_ref, payload_ref, 0)
-    pack(from_ref, weights_ref, payload_ref, BS)
-    left = lax.broadcasted_iota(jnp.int32, (8, LANE), 1) < BS
-    for o in range(TILES):
-        slots = [jnp.full((8, LANE), slots_ref[2 * o + k], jnp.int32) for k in range(2)]
-        payload_ref[o, pl.ds(2 * BS, 8), :] = jnp.where(left, slots[0], slots[1]).astype(f32).astype(bf16)
+    left = lax.broadcasted_iota(jnp.int32, (BS, LANE), 1) < BS
+    for part in range(4):
+        for o in range(part * 8, part * 8 + 8):
+            source = [from_ref[2 * o + k] for k in range(2)]
+            payload_ref[o] = jnp.where(left, blocks_ref[source[0]], blocks_ref[source[1]])
+        owners = pl.ds(part * 8, 8)
+        stores.append(load(6 + part, payload_ref.at[owners], payload_hbm.at[owners, pl.ds(0, BS), :]))
+    for store in stores:
+        store.wait()
 
 
 def sum_kernel(arrived_ref, total_ref):
@@ -221,47 +277,70 @@
     coadd_weight,
 ):
     sds = jax.ShapeDtypeStruct
-    tiles = template[0, 0].reshape(H // 8, 8, CB, LANE)
-    tiles = with_layout_constraint(tiles, Layout(major_to_minor=(0, 2, 1, 3)))
-    held = all_to_all(tiles.transpose(0, 2, 1, 3).reshape(TILES, 16, LANE))
-    outgoing = call(
-        roll_kernel, sds((TILES, VISITS * 16, LANE), bf16), [SMEM, VMEM], (0, 400_000)
-    )(visit_offset, held)
-
-    outgoing, index = lax.optimization_barrier((outgoing, kernel_index.T))
-    band, both, origin, slots = call(
+    blocks = pltpu.VMEM((NBLK + 1, BS, LANE), bf16)
+    prep = call(
         prep_kernel,
         (
             sds((NB * LANE, 2 * LANE), bf16),
-            sds((VISITS, 4 * H, NB * H), bf16),
+            sds((8 * NB, LANE), f32),
             sds((2 * TILES,), jnp.int32),
             sds((2 * TILES,), jnp.int32),
         ),
-        [SMEM, SMEM, SMEM, SMEM, VMEM, VMEM],
-        (10_000_000, 3_000_000),
+        [SMEM] * 3 + [VMEM] * 3,
+        (10_000_000, 1_000_000),
         [
             pltpu.SMEM((TILES,), jnp.int32),
-            pltpu.VMEM((NB, 2 * LANE), f32),
-            pltpu.VMEM((8, LANE), f32),
-            pltpu.VMEM((NB, 8, 2 * LANE), f32),
+            pltpu.VMEM((LANE, 2 * LANE), f32),
+            pltpu.VMEM((16, LANE), f32),
         ],
         (VMEM, VMEM, SMEM, SMEM),
-    )(index, block_owner[0, 0], block_slot[0, 0], block_count[0, 0], filters, spatial_coeff[0, 0])
-    arrived = all_to_all(outgoing)
-
-    blocks = pltpu.VMEM((NBLK + 1, BS, LANE), bf16)
+    )
+    second_prep = call(
+        second_prep_kernel,
+        (sds((VISITS, 4 * H, NB * H), bf16), sds((TILES, BS + 8, LANE), bf16)),
+        [SMEM, SMEM, VMEM, VMEM],
+        (10_000_000, 3_000_000),
+        [blocks],
+    )
+
+    def shifted(d, beside):
+        pairs = [((i + d) % TILES, i) for i in range(TILES)]
+
+        def branch(tile, args):
+            return (lax.ppermute(tile, "tile", pairs) if d else tile), beside(*args)
+
+        return branch
+
+    own = template[0, 0]
+    tables = (kernel_index.T, filters, spatial_coeff[0, 0].transpose(1, 0, 2))
+    places = (block_owner[0, 0], block_slot[0, 0], block_count[0, 0])
+    first, (band, eff, origin, slots) = lax.switch(
+        visit_offset[0, 0], [shifted(d, prep) for d in range(TILES)], own, places + tables
+    )
+    second, (both, weights) = lax.switch(
+        visit_offset[0, 1],
+        [shifted(d, second_prep) for d in range(TILES)],
+        own,
+        (origin, slots, eff, inverse_variance[0, 0]),
+    )
+
     difference, payload = call(
         main_kernel,
         (sds((VISITS, H, W), f32), sds((TILES, 2 * BS + 8, LANE), bf16)),
-        [SMEM, SMEM] + [VMEM] * 5,
+        [SMEM] + [VMEM] * 4 + [ANY] * 3,
         (2_000_000_000, 6_000_000),
         [
             pltpu.VMEM((VISITS * CB * H, 2 * LANE), bf16),
             pltpu.VMEM((VISITS, NB * H, W), bf16),
             blocks,
-            blocks,
+            pltpu.VMEM((VISITS, H, W), f32),
+            pltpu.VMEM((VISITS, H, W), bf16),
+            pltpu.VMEM((VISITS, H, W), f32),
+            pltpu.VMEM((TILES, BS, LANE), bf16),
+            pltpu.SemaphoreType.DMA((10,)),
         ],
-    )(origin, slots, arrived, band, both, science[0, 0], inverse_variance[0, 0])
+        (ANY, ANY),
+    )(origin, first, second, band, both, weights, science[0, 0], inverse_variance[0, 0])
 
     total = call(
         sum_kernel, sds((PATCHES, BS, LANE), f32), [VMEM], (5_000_000, 1_300_000)

time: 70.7 us -> 66.5 us (0.941)
  blocking collectives: 37.4 us -> 23.7 us
  starting transfers between devices: 9.92 us -> 17.4 us
  Pallas kernels: 8.91 us -> 12.4 us
  local copies, waits for them, and re-layouts: 4.4 us -> 2.3 us
  between operations: 0.73 us -> 2.05 us
  waiting for transfers between devices: 8.91 us -> 7.93 us
    all_to_all x2 -> x1, blocking collectives: 37.4 us -> 23.7 us  [all_to_all(): return lax.all_to_all(x, 'tile', split_axis=0, concat_axis=0, tiled=True)]
    ppermute x0 -> x2, starting transfers between devices: none -> 8.74 us  [branch(): return (lax.ppermute(tile, 'tile', pairs) if d else tile, beside(*args))]
    all_to_all x1 -> x0, starting transfers between devices: 3.87 us -> none  [all_to_all(): return lax.all_to_all(x, 'tile', split_axis=0, concat_axis=0, tiled=True)]
    all_to_all x1 -> x0, waiting for transfers between devices: 3.83 us -> none  [all_to_all(): return lax.all_to_all(x, 'tile', split_axis=0, concat_axis=0, tiled=True)]
    pallas_call x2, Pallas kernels: 3.69 us -> 6.73 us  [branch(): return (lax.ppermute(tile, 'tile', pairs) if d else tile, beside(*args))]
    ppermute x0 -> x2, waiting for transfers between devices: none -> 2.85 us  [branch(): return (lax.ppermute(tile, 'tile', pairs) if d else tile, beside(*args))]
    unnamed x20 -> x9, local copies, waits for them, and re-layouts: 3.71 us -> 0.97 us
    ppermute x1, starting transfers between devices: 4.13 us -> 6.75 us  [shards(): high = lax.ppermute(total[0], 'sky', [(i + 1, i) for i in range(count - 1)])]
  transfers between devices with their start and end apart: 3 -> 4, of which waited for: 2 -> 2; matrix products, arithmetic and copies ran while one was open for 1% -> 0% of each run, Pallas kernels for 3% -> 10%
where the time goes in v3:
time: 66.5 us; the launch traced here: 66.1 us
  blocking collectives  23.7 us (36%)
  starting transfers between devices  17.4 us (26%)
  Pallas kernels  12.4 us (19%)
  waiting for transfers between devices  7.93 us (12%)
  local copies, waits for them, and re-layouts  2.3 us (3%)
  between operations  2.05 us (3%)
    all_to_all x1, blocking collectives, all_to_all(): return lax.all_to_all(x, 'tile', split_axis=0, concat_axis=0, tiled=True)  23.7 us
    ppermute x2, starting transfers between devices, branch(): return (lax.ppermute(tile, 'tile', pairs) if d else tile, beside(*args))  8.74 us
    ppermute x1, starting transfers between devices, shards(): high = lax.ppermute(total[0], 'sky', [(i + 1, i) for i in range(count - 1)])  6.75 us
    pallas_call x2, Pallas kernels, branch(): return (lax.ppermute(tile, 'tile', pairs) if d else tile, beside(*args))  6.73 us
    ppermute x1, waiting for transfers between devices, shards(): lax.ppermute(total[PATCHES - 1], 'sky', [(i, i + 1) for i in range(count...  5.08 us
    pallas_call x1, Pallas kernels, shards(): call(main_kernel, (sds((VISITS, H, W), f32), sds((TILES, 2 * BS + 8, LANE...  4.05 us
    ppermute x2, waiting for transfers between devices, branch(): return (lax.ppermute(tile, 'tile', pairs) if d else tile, beside(*args))  2.85 us
    ppermute x1, starting transfers between devices, shards(): lax.ppermute(total[PATCHES - 1], 'sky', [(i, i + 1) for i in range(count...  1.92 us
  transfers between devices with their start and end apart: 4, of which 2 were waited for; matrix products, arithmetic and copies ran while one was open for 0% of the time, Pallas kernels for 10%

profile of v3, /device:TPU:384, one launch (start us, length us, event | category | flops | bytes accessed | tf_op | source)
XLA Modules:
  0.0 66.1 jit_solution(337807805154964042)
XLA Ops:
  0.6 0.0 copy-start.3
  0.6 0.9 %copy.273 = bf16[1,1,128,512]{3,2,1,0:T(8,128)(2,1)S(1)} copy(bf16[1,1,128,512]{3,2,1,0:T(8,128)(2,1)} %param.78) | data formatting | bytes 262144
  1.6 1.3 %fusion = (s32[1,1]{1,0:T(1,128)}, s32[1,1]{1,0:T(1,128)}) fusion(s32[1,2]{1,0:T(1,128)} %param.82), kind=kLoop, calls=%fused_computation.2 | loop fusion | bytes 16 | tf_op jit(solution)/shard_map/slice | solution.py:321
  3.6 8.0 %conditional.2 = (bf16[128,512]{1,0:T(8,128)(2,1)}, bf16[1024,256]{1,0:T(8,128)(2,1)}, f32[64,128]{1,0:T(8,128)S(1)}, s32[64]{0:T(128)S(1)}, s32[64]{0:T(128)S(1)}) conditional(s32[]{:T(128)} %bitcast, (s32[32]{0:T(128)}, s32[32]{0:T(128)}, s32[2]{0:T(128)}, s32[2,20]{1,0:T(2,128)}, bf16[8,21]{1,0:T(8,128)(2,1)}, ...), branch_computations={%region_0.0_spmd, %region_1.0_spmd, %region_2.0_spmd, %region_3.0_... | conditional | flops 10000000 | bytes 1524368 | solution.py:317
  3.6 4.9 %collective-permute-start.7 = (bf16[128,512]{1,0:T(8,128)(2,1)S(1)}, bf16[128,512]{1,0:T(8,128)(2,1)}, u32[]{:S(2)}, u32[]{:S(2)}) collective-permute-start(bf16[128,512]{1,0:T(8,128)(2,1)S(1)} %get-tuple-element.856), channel_id=1, source_target_pairs={{8,0},{9,1},{10,2},{11,3},{12,4},{13,5},{14,6},{15,7},{16,8},{17,9... | collective-permute-start | bytes 393224 | tf_op jit(solution)/shard_map/cond/branch_8_fun/ppermute | solution.py:310
  8.5 2.8 %branch_8_fun.2 = (bf16[1024,256]{1,0:T(8,128)(2,1)}, f32[64,128]{1,0:T(8,128)S(1)}, s32[64]{0:T(128)S(1)}, s32[64]{0:T(128)S(1)}) custom-call(s32[32]{0:T(128)} %get-tuple-element.857.owner_ref, s32[32]{0:T(128)} %get-tuple-element.858.slot_ref, s32[2]{0:T(128)} %get-tuple-element.859.count_ref, s32[2,20]{1,0:T(2,128)} %get-tuple-element.860.index_ref, ...), custom_call_target="tpu_custom_call" | custom-call | flops 10000000 | bytes 1000000 | tf_op jit(solution)/shard_map/cond/branch_8_fun/pallas_call | solution.py:310
  11.3 0.0 collective-permute-done.7
  12.2 0.0 copy-done.3
  12.2 0.0 copy-start.2
  12.2 10.7 %conditional.3 = (bf16[128,512]{1,0:T(8,128)(2,1)S(1)}, bf16[2,512,1024]{2,1,0:T(8,128)(2,1)S(1)}, bf16[32,72,128]{2,1,0:T(8,128)(2,1)S(1)}) conditional(s32[]{:T(128)} %bitcast.9, (s32[64]{0:T(128)S(1)}, s32[64]{0:T(128)S(1)}, f32[64,128]{1,0:T(8,128)S(1)}, bf16[2,128,512]{2,1,0:T(8,128)(2,1)S(1)}, ...), branch_computations={%region_32.0_spmd, %region_33.0_spmd, %region_34.0_spmd, %region_3... | conditional | flops 10000000 | bytes 3786496 | solution.py:320
  12.3 3.8 %collective-permute-start.52 = (bf16[128,512]{1,0:T(8,128)(2,1)S(1)}, bf16[128,512]{1,0:T(8,128)(2,1)S(1)}, u32[]{:S(2)}, u32[]{:S(2)}) collective-permute-start(bf16[128,512]{1,0:T(8,128)(2,1)S(1)} %get-tuple-element.1274), channel_id=1, source_target_pairs={{22,0},{23,1},{24,2},{25,3},{26,4},{27,5},{28,6},{29,7},{30,8},{31... | collective-permute-start | bytes 393224 | tf_op jit(solution)/shard_map/cond/branch_22_fun/ppermute | solution.py:310
  16.1 3.9 %branch_22_fun.3 = (bf16[2,512,1024]{2,1,0:T(8,128)(2,1)S(1)}, bf16[32,72,128]{2,1,0:T(8,128)(2,1)S(1)}) custom-call(s32[64]{0:T(128)S(1)} %get-tuple-element.1275.from_ref, s32[64]{0:T(128)S(1)} %get-tuple-element.1276.slots_ref, f32[64,128]{1,0:T(8,128)S(1)} %get-tuple-element.1277.eff_ref, bf16[2,128,512]{2,1,0:T(8,128)(2,1)S(1)} %get-tuple-element.1278.inverse_ref), custom_call_target="tpu_custom_call" | custom-call | flops 10000000 | bytes 3000000 | tf_op jit(solution)/shard_map/cond/branch_22_fun/pallas_call | solution.py:310
  20.0 2.8 %collective-permute-done.52 = bf16[128,512]{1,0:T(8,128)(2,1)S(1)} collective-permute-done((bf16[128,512]{1,0:T(8,128)(2,1)S(1)}, bf16[128,512]{1,0:T(8,128)(2,1)S(1)}, u32[]{:S(2)}, u32[]{:S(2)}) %collective-permute-start.52) | collective-permute-done | bytes 131104 | tf_op jit(solution)/shard_map/cond/branch_22_fun/ppermute | solution.py:310
  22.9 4.1 %shard_map.131 = (f32[2,128,512]{2,1,0:T(8,128)}, bf16[32,136,128]{2,1,0:T(8,128)(2,1)S(1)}) custom-call(s32[64]{0:T(128)S(1)} %get-tuple-element.1356.from_ref, bf16[128,512]{1,0:T(8,128)(2,1)} %get-tuple-element.1357.tile0_ref, bf16[128,512]{1,0:T(8,128)(2,1)S(1)} %get-tuple-element.1360.tile1_ref, bf16[1024,256]{1,0:T(8,128)(2,1)} %get-tuple-element.1361.band_ref, ...), custom_call_target="tpu_custom_call" | custom-call | flops 2000000000 | bytes 6000000 | tf_op jit(solution)/shard_map/pallas_call | solution.py:327
  27.0 0.0 copy-start
  27.0 0.0 copy-start.1
  27.0 23.7 %all_to_all.5.arrived_ref = bf16[32,136,128]{2,1,0:T(8,128)(2,1)S(1)} all-to-all(bf16[32,136,128]{2,1,0:T(8,128)(2,1)S(1)} %get-tuple-element.1365), channel_id=1, replica_groups=mesh['sky'=16,'tile'=32] {'tile'}, dimensions={0} | all-to-all | bytes 2228224 | tf_op jit(solution)/shard_map/all_to_all | solution.py:262
  50.7 0.9 %shard_map.132.total_ref = f32[3,64,128]{2,1,0:T(8,128)S(1)} custom-call(bf16[32,136,128]{2,1,0:T(8,128)(2,1)S(1)} %all_to_all.5.arrived_ref), custom_call_target="tpu_custom_call" | custom-call | flops 5000000 | bytes 1300000 | tf_op jit(solution)/shard_map/pallas_call | solution.py:345
  51.6 6.8 %collective-permute-start.63 = (f32[64,128]{1,0:T(8,128)S(1)}, f32[64,128]{1,0:T(8,128)S(1)}, u32[]{:S(2)}, u32[]{:S(2)}) collective-permute-start(f32[64,128]{1,0:T(8,128)S(1)} %get-tuple-element.1370), channel_id=1, source_target_pairs={{32,0},{64,32},{96,64},{128,96},{160,128},{192,160},{224,192},{256... | collective-permute-start | bytes 98312 | tf_op jit(solution)/shard_map/ppermute | solution.py:351
  58.3 1.9 %collective-permute-start.62 = (f32[64,128]{1,0:T(8,128)S(1)}, f32[64,128]{1,0:T(8,128)S(1)}, u32[]{:S(2)}, u32[]{:S(2)}) collective-permute-start(f32[64,128]{1,0:T(8,128)S(1)} %get-tuple-element.1371), channel_id=1, source_target_pairs={{0,32},{32,64},{64,96},{96,128},{128,160},{160,192},{192,224},{224... | collective-permute-start | bytes 98312 | tf_op jit(solution)/shard_map/ppermute | solution.py:350
  60.3 0.0 collective-permute-done.63.high_ref
  60.3 5.1 %collective-permute-done.62.low_ref = f32[64,128]{1,0:T(8,128)S(1)} collective-permute-done((f32[64,128]{1,0:T(8,128)S(1)}, f32[64,128]{1,0:T(8,128)S(1)}, u32[]{:S(2)}, u32[]{:S(2)}) %collective-permute-start.62) | collective-permute-done | bytes 32800 | tf_op jit(solution)/shard_map/ppermute | solution.py:350
  65.4 0.0 copy-done
  65.4 0.7 %shard_map.133 = f32[3,32,128]{2,1,0:T(8,128)} custom-call(f32[3,64,128]{2,1,0:T(8,128)S(1)} %shard_map.132.total_ref, f32[64,128]{1,0:T(8,128)S(1)} %collective-permute-done.62.low_ref, f32[64,128]{1,0:T(8,128)S(1)} %collective-permute-done.63.high_ref, f32[3,32,128]{2,1,0:T(8,128)S(1)} %bitcast.20, f32[3,32,128]{2,1,0:T(8,128)S(1)} %bitcast.21), custom_call_target="tpu_custom_call" | custom-call | flops 100000 | bytes 300000 | tf_op jit(solution)/shard_map/pallas_call | solution.py:352
  (4 shorter events, 0.0 us)
Async XLA Ops:
  0.6 11.6 %copy-start.3 = (bf16[1,1,2,128,512]{4,3,2,1,0:T(8,128)(2,1)S(1)}, bf16[1,1,2,128,512]{4,3,2,1,0:T(8,128)(2,1)}, u32[]{:S(2)}) copy-start(bf16[1,1,2,128,512]{4,3,2,1,0:T(8,128)(2,1)} %param.77) | copy-start | bytes 786436
  3.6 7.7 %collective-permute-start.7 = (bf16[128,512]{1,0:T(8,128)(2,1)S(1)}, bf16[128,512]{1,0:T(8,128)(2,1)}, u32[]{:S(2)}, u32[]{:S(2)}) collective-permute-start(bf16[128,512]{1,0:T(8,128)(2,1)S(1)} %get-tuple-element.856), channel_id=1, source_target_pairs={{8,0},{9,1},{10,2},{11,3},{12,4},{13,5},{14,6},{15,7},{16,8},{17,9... | collective-permute-start | bytes 393224 | tf_op jit(solution)/shard_map/cond/branch_8_fun/ppermute | solution.py:310
  12.2 10.7 %copy-start.2 = (f32[1,1,2,128,512]{4,3,2,1,0:T(8,128)S(1)}, f32[1,1,2,128,512]{4,3,2,1,0:T(8,128)}, u32[]{:S(2)}) copy-start(f32[1,1,2,128,512]{4,3,2,1,0:T(8,128)} %param.76) | copy-start | bytes 1572868
  12.3 10.6 %collective-permute-start.52 = (bf16[128,512]{1,0:T(8,128)(2,1)S(1)}, bf16[128,512]{1,0:T(8,128)(2,1)S(1)}, u32[]{:S(2)}, u32[]{:S(2)}) collective-permute-start(bf16[128,512]{1,0:T(8,128)(2,1)S(1)} %get-tuple-element.1274), channel_id=1, source_target_pairs={{22,0},{23,1},{24,2},{25,3},{26,4},{27,5},{28,6},{29,7},{30,8},{31... | collective-permute-start | bytes 393224 | tf_op jit(solution)/shard_map/cond/branch_22_fun/ppermute | solution.py:310
  27.0 38.4 %copy-start = (f32[1,1,3,4096]{3,1,2,0:T(1,128)S(1)}, f32[1,1,3,4096]{3,1,2,0:T(1,128)}, u32[]{:S(2)}) copy-start(f32[1,1,3,4096]{3,1,2,0:T(1,128)} %param.86) | copy-start | bytes 147460
  27.0 38.4 %copy-start.1 = (f32[1,1,3,4096]{3,1,2,0:T(1,128)S(1)}, f32[1,1,3,4096]{3,1,2,0:T(1,128)}, u32[]{:S(2)}) copy-start(f32[1,1,3,4096]{3,1,2,0:T(1,128)} %param.87) | copy-start | bytes 147460
  51.6 8.7 %collective-permute-start.63 = (f32[64,128]{1,0:T(8,128)S(1)}, f32[64,128]{1,0:T(8,128)S(1)}, u32[]{:S(2)}, u32[]{:S(2)}) collective-permute-start(f32[64,128]{1,0:T(8,128)S(1)} %get-tuple-element.1370), channel_id=1, source_target_pairs={{32,0},{64,32},{96,64},{128,96},{160,128},{192,160},{224,192},{256... | collective-permute-start | bytes 98312 | tf_op jit(solution)/shard_map/ppermute | solution.py:351
  58.3 7.0 %collective-permute-start.62 = (f32[64,128]{1,0:T(8,128)S(1)}, f32[64,128]{1,0:T(8,128)S(1)}, u32[]{:S(2)}, u32[]{:S(2)}) collective-permute-start(f32[64,128]{1,0:T(8,128)S(1)} %get-tuple-element.1371), channel_id=1, source_target_pairs={{0,32},{32,64},{64,96},{96,128},{128,160},{160,192},{192,224},{224... | collective-permute-start | bytes 98312 | tf_op jit(solution)/shard_map/ppermute | solution.py:350

commit v4 on v3

--- a/solution.py
+++ b/solution.py
@@ -27,14 +27,14 @@
 SMEM = pl.BlockSpec(memory_space=pltpu.SMEM)
 
 
-def call(kernel, outs, in_specs, cost, scratch=(), out_specs=None):
+def call(kernel, outs, in_specs, cost, scratch=(), out_specs=None, vmem_mib=24):
     return pl.pallas_call(
         kernel,
         out_shape=outs,
         in_specs=in_specs,
         out_specs=out_specs or jax.tree.map(lambda _: VMEM, outs),
         scratch_shapes=list(scratch),
-        compiler_params=pltpu.CompilerParams(vmem_limit_bytes=24 * 2**20),
+        compiler_params=pltpu.CompilerParams(vmem_limit_bytes=vmem_mib * 2**20),
         cost_estimate=pl.CostEstimate(flops=cost[0], bytes_accessed=cost[1], transcendentals=0),
     )
 
@@ -111,7 +111,7 @@
 
 def prep_kernel(
     owner_ref, slot_ref, count_ref, index_ref, filters_ref, coeff_ref,
-    band_ref, eff_ref, from_ref, slots_ref, seen_ref, taps_ref, weight_ref,
+    eff_ref, taps_ref, from_ref, slots_ref, seen_ref, weight_ref,
 ):
     def clear(o, carry):
         from_ref[2 * o] = NBLK
@@ -138,15 +138,16 @@
 
         lax.fori_loop(0, BPV, put, 0, unroll=2)
 
+
+def second_prep_kernel(
+    from_ref, slots_ref, eff_ref, taps_ref, inverse_ref, band_ref, both_ref, payload_ref, blocks_ref
+):
     def band(j, carry):
         rows = pl.ds(pl.multiple_of(j * LANE, LANE), LANE)
         band_ref[rows, :] = toeplitz(taps_ref[pl.ds(j, 1), :], 2 * LANE).astype(bf16)
         return carry
 
     lax.fori_loop(0, NB, band, 0, unroll=2)
-
-
-def second_prep_kernel(from_ref, slots_ref, eff_ref, inverse_ref, both_ref, payload_ref, blocks_ref):
     column_bands(eff_ref, both_ref)
     pack_weights(from_ref, slots_ref, inverse_ref, payload_ref, blocks_ref)
 
@@ -160,6 +161,12 @@
             r = v * BPV + by * (W // BS) + pair * 2
             blocks_ref[r] = jnp.where(left, here, there).astype(bf16)
             blocks_ref[r + 1] = jnp.where(left, there, here).astype(bf16)
+
+
+def stay_kernel(tile_hbm, out_hbm, sem):
+    copy = pltpu.make_async_copy(tile_hbm, out_hbm, sem)
+    copy.start()
+    copy.wait()
 
 
 def main_kernel(
@@ -203,9 +210,9 @@
                     filtered_ref[v, pl.ds((2 * jj + j) * H, H), pl.ds(b * LANE, LANE)] = rows[
                         top : top + H, j * LANE : (j + 1) * LANE
                     ]
-    for copy in loads:
+    for copy in loads[:-1]:
         copy.wait()
-    stores = []
+    stores = loads[-1:]
     for v in range(VISITS):
         both = jnp.dot(both_ref[v], filtered_ref[v], preferred_element_type=f32)
         both = both[: 2 * H] + both[2 * H :]
@@ -281,8 +288,8 @@
     prep = call(
         prep_kernel,
         (
-            sds((NB * LANE, 2 * LANE), bf16),
             sds((8 * NB, LANE), f32),
+            sds((LANE, 2 * LANE), f32),
             sds((2 * TILES,), jnp.int32),
             sds((2 * TILES,), jnp.int32),
         ),
@@ -290,38 +297,45 @@
         (10_000_000, 1_000_000),
         [
             pltpu.SMEM((TILES,), jnp.int32),
-            pltpu.VMEM((LANE, 2 * LANE), f32),
             pltpu.VMEM((16, LANE), f32),
         ],
         (VMEM, VMEM, SMEM, SMEM),
     )
     second_prep = call(
         second_prep_kernel,
-        (sds((VISITS, 4 * H, NB * H), bf16), sds((TILES, BS + 8, LANE), bf16)),
-        [SMEM, SMEM, VMEM, VMEM],
+        (
+            sds((NB * LANE, 2 * LANE), bf16),
+            sds((VISITS, 4 * H, NB * H), bf16),
+            sds((TILES, BS + 8, LANE), bf16),
+        ),
+        [SMEM, SMEM] + [VMEM] * 3,
         (10_000_000, 3_000_000),
         [blocks],
     )
 
+    stay = call(
+        stay_kernel, sds((H, W), bf16), [ANY], (0, 300_000), [pltpu.SemaphoreType.DMA], ANY
+    )
+
     def shifted(d, beside):
         pairs = [((i + d) % TILES, i) for i in range(TILES)]
 
         def branch(tile, args):
-            return (lax.ppermute(tile, "tile", pairs) if d else tile), beside(*args)
+            return (lax.ppermute(tile, "tile", pairs) if d else stay(tile)), beside(*args)
 
         return branch
 
     own = template[0, 0]
     tables = (kernel_index.T, filters, spatial_coeff[0, 0].transpose(1, 0, 2))
     places = (block_owner[0, 0], block_slot[0, 0], block_count[0, 0])
-    first, (band, eff, origin, slots) = lax.switch(
+    first, (eff, taps, origin, slots) = lax.switch(
         visit_offset[0, 0], [shifted(d, prep) for d in range(TILES)], own, places + tables
     )
-    second, (both, weights) = lax.switch(
+    second, (band, both, weights) = lax.switch(
         visit_offset[0, 1],
         [shifted(d, second_prep) for d in range(TILES)],
         own,
-        (origin, slots, eff, inverse_variance[0, 0]),
+        (origin, slots, eff, taps, inverse_variance[0, 0]),
     )
 
     difference, payload = call(

time: 66.5 us -> 64.7 us (0.973)
  the two profiles are of different devices: /device:TPU:384 before, /device:TPU:64 now
where the time goes in v4:
time: 64.7 us; the launch traced here: 64 us
  blocking collectives  24.2 us (37%)
  starting transfers between devices  21.1 us (33%)
  Pallas kernels  12 us (19%)
  waiting for transfers between devices  3.1 us (5%)
  between operations  2.02 us (3%)
  local copies, waits for them, and re-layouts  1.34 us (2%)
    all_to_all x1, blocking collectives, all_to_all(): return lax.all_to_all(x, 'tile', split_axis=0, concat_axis=0, tiled=True)  24.2 us
    ppermute x2, starting transfers between devices, branch(): lax.ppermute(tile, 'tile', pairs)  15.2 us
    pallas_call x2, Pallas kernels, branch(): beside(*args)  6.51 us
    pallas_call x1, Pallas kernels, shards(): call(main_kernel, (sds((VISITS, H, W), f32), sds((TILES, 2 * BS + 8, LANE...  3.9 us
    ppermute x1, starting transfers between devices, shards(): lax.ppermute(total[PATCHES - 1], 'sky', [(i, i + 1) for i in range(count...  3.56 us
    ppermute x1, starting transfers between devices, shards(): high = lax.ppermute(total[0], 'sky', [(i + 1, i) for i in range(count - 1)])  2.28 us
    ppermute x1, waiting for transfers between devices, shards(): lax.ppermute(total[PATCHES - 1], 'sky', [(i, i + 1) for i in range(count...  2.23 us
    slice x1, local copies, waits for them, and re-layouts, shards(): visit_offset[0, 1]  1.31 us
  transfers between devices with their start and end apart: 4, of which 2 were waited for; matrix products, arithmetic and copies ran while one was open for 0% of the time, Pallas kernels for 10%

profile of v4, /device:TPU:64, one launch (start us, length us, event | category | flops | bytes accessed | tf_op | source)
XLA Modules:
  0.0 64.0 jit_solution(11780680251150816650)
XLA Ops:
  0.6 0.0 copy-start.3
  0.6 1.3 %fusion = (s32[1,1]{1,0:T(1,128)}, s32[1,1]{1,0:T(1,128)}) fusion(s32[1,2]{1,0:T(1,128)} %param.82), kind=kLoop, calls=%fused_computation.2 | loop fusion | bytes 16 | tf_op jit(solution)/shard_map/slice | solution.py:335
  3.3 10.5 %conditional.2 = (bf16[128,512]{1,0:T(8,128)(2,1)}, f32[64,128]{1,0:T(8,128)S(1)}, f32[128,256]{1,0:T(8,128)S(1)}, s32[64]{0:T(128)S(1)}, s32[64]{0:T(128)S(1)}) conditional(s32[]{:T(128)} %bitcast, (bf16[128,512]{1,0:T(8,128)(2,1)}, s32[32]{0:T(128)}, s32[32]{0:T(128)}, s32[2]{0:T(128)}, s32[2,20]{1,0:T(2,128)}, ...), branch_computations={%region_0.0_spmd, %region_1.0_spmd, %region_2.0_spmd, %region_3.0_... | conditional | flops 10000000 | bytes 1524368 | solution.py:331
  3.3 7.4 %collective-permute-start.3 = (bf16[128,512]{1,0:T(8,128)(2,1)}, bf16[128,512]{1,0:T(8,128)(2,1)}, u32[]{:S(2)}, u32[]{:S(2)}) collective-permute-start(bf16[128,512]{1,0:T(8,128)(2,1)} %get-tuple-element.876), channel_id=1, source_target_pairs={{4,0},{5,1},{6,2},{7,3},{8,4},{9,5},{10,6},{11,7},{12,8},{13,9},{1... | collective-permute-start | bytes 393224 | tf_op jit(solution)/shard_map/cond/branch_4_fun/ppermute | solution.py:324
  10.7 2.2 %branch_4_fun.2 = (f32[64,128]{1,0:T(8,128)S(1)}, f32[128,256]{1,0:T(8,128)S(1)}, s32[64]{0:T(128)S(1)}, s32[64]{0:T(128)S(1)}) custom-call(s32[32]{0:T(128)} %get-tuple-element.877.owner_ref, s32[32]{0:T(128)} %get-tuple-element.878.slot_ref, s32[2]{0:T(128)} %get-tuple-element.879.count_ref, s32[2,20]{1,0:T(2,128)} %get-tuple-element.880.index_ref, ...), custom_call_target="tpu_custom_call" | custom-call | flops 10000000 | bytes 1000000 | tf_op jit(solution)/shard_map/cond/branch_4_fun/pallas_call | solution.py:324
  12.9 0.9 %collective-permute-done.3 = bf16[128,512]{1,0:T(8,128)(2,1)} collective-permute-done((bf16[128,512]{1,0:T(8,128)(2,1)}, bf16[128,512]{1,0:T(8,128)(2,1)}, u32[]{:S(2)}, u32[]{:S(2)}) %collective-permute-start.3) | collective-permute-done | bytes 131104 | tf_op jit(solution)/shard_map/cond/branch_4_fun/ppermute | solution.py:324
  13.7 0.0 copy-done.3
  13.7 12.4 %conditional.3 = (bf16[128,512]{1,0:T(8,128)(2,1)}, bf16[1024,256]{1,0:T(8,128)(2,1)S(1)}, bf16[2,512,1024]{2,1,0:T(8,128)(2,1)S(1)}, bf16[32,72,128]{2,1,0:T(8,128)(2,1)S(1)}) conditional(s32[]{:T(128)} %bitcast.8, (bf16[128,512]{1,0:T(8,128)(2,1)}, s32[64]{0:T(128)S(1)}, s32[64]{0:T(128)S(1)}, ...), branch_computations={%region_32.0_spmd, %region_33.0_spmd, %region_34.0_spmd, %region_3... | conditional | flops 10000000 | bytes 3524360 | solution.py:334
  13.7 7.9 %collective-permute-start.32 = (bf16[128,512]{1,0:T(8,128)(2,1)}, bf16[128,512]{1,0:T(8,128)(2,1)}, u32[]{:S(2)}, u32[]{:S(2)}) collective-permute-start(bf16[128,512]{1,0:T(8,128)(2,1)} %get-tuple-element.1202), channel_id=1, source_target_pairs={{2,0},{3,1},{4,2},{5,3},{6,4},{7,5},{8,6},{9,7},{10,8},{11,9},{12,... | collective-permute-start | bytes 393224 | tf_op jit(solution)/shard_map/cond/branch_2_fun/ppermute | solution.py:324
  21.6 4.3 %branch_2_fun.3 = (bf16[1024,256]{1,0:T(8,128)(2,1)S(1)}, bf16[2,512,1024]{2,1,0:T(8,128)(2,1)S(1)}, bf16[32,72,128]{2,1,0:T(8,128)(2,1)S(1)}) custom-call(s32[64]{0:T(128)S(1)} %get-tuple-element.1203.from_ref, s32[64]{0:T(128)S(1)} %get-tuple-element.1204.slots_ref, f32[64,128]{1,0:T(8,128)S(1)} %get-tuple-element.1205.eff_ref, ...), custom_call_target="tpu_custom_call" | custom-call | flops 10000000 | bytes 3000000 | tf_op jit(solution)/shard_map/cond/branch_2_fun/pallas_call | solution.py:324
  26.0 0.0 collective-permute-done.32
  26.2 0.0 copy-done.2
  26.2 3.9 %shard_map.131 = (f32[2,128,512]{2,1,0:T(8,128)}, bf16[32,136,128]{2,1,0:T(8,128)(2,1)S(1)}) custom-call(s32[64]{0:T(128)S(1)} %get-tuple-element.1485.from_ref, bf16[128,512]{1,0:T(8,128)(2,1)} %get-tuple-element.1486.tile0_ref, bf16[128,512]{1,0:T(8,128)(2,1)} %get-tuple-element.1490.tile1_ref, bf16[1024,256]{1,0:T(8,128)(2,1)S(1)} %get-tuple-element.1491.band_ref, ...), custom_call_target="tpu_custom_call" | custom-call | flops 2000000000 | bytes 6000000 | tf_op jit(solution)/shard_map/pallas_call | solution.py:341
  30.1 0.0 copy-start
  30.1 0.0 copy-start.1
  30.1 24.2 %all_to_all.5.arrived_ref = bf16[32,136,128]{2,1,0:T(8,128)(2,1)S(1)} all-to-all(bf16[32,136,128]{2,1,0:T(8,128)(2,1)S(1)} %get-tuple-element.1495), channel_id=1, replica_groups=mesh['sky'=16,'tile'=32] {'tile'}, dimensions={0} | all-to-all | bytes 2228224 | tf_op jit(solution)/shard_map/all_to_all | solution.py:269
  54.3 0.9 %shard_map.132.total_ref = f32[3,64,128]{2,1,0:T(8,128)S(1)} custom-call(bf16[32,136,128]{2,1,0:T(8,128)(2,1)S(1)} %all_to_all.5.arrived_ref), custom_call_target="tpu_custom_call" | custom-call | flops 5000000 | bytes 1300000 | tf_op jit(solution)/shard_map/pallas_call | solution.py:359
  55.2 2.3 %collective-permute-start.63 = (f32[64,128]{1,0:T(8,128)S(1)}, f32[64,128]{1,0:T(8,128)S(1)}, u32[]{:S(2)}, u32[]{:S(2)}) collective-permute-start(f32[64,128]{1,0:T(8,128)S(1)} %get-tuple-element.1500), channel_id=1, source_target_pairs={{32,0},{64,32},{96,64},{128,96},{160,128},{192,160},{224,192},{256... | collective-permute-start | bytes 98312 | tf_op jit(solution)/shard_map/ppermute | solution.py:365
  57.5 3.6 %collective-permute-start.62 = (f32[64,128]{1,0:T(8,128)S(1)}, f32[64,128]{1,0:T(8,128)S(1)}, u32[]{:S(2)}, u32[]{:S(2)}) collective-permute-start(f32[64,128]{1,0:T(8,128)S(1)} %get-tuple-element.1501), channel_id=1, source_target_pairs={{0,32},{32,64},{64,96},{96,128},{128,160},{160,192},{192,224},{224... | collective-permute-start | bytes 98312 | tf_op jit(solution)/shard_map/ppermute | solution.py:364
  61.1 0.0 collective-permute-done.63.high_ref
  61.1 2.2 %collective-permute-done.62.low_ref = f32[64,128]{1,0:T(8,128)S(1)} collective-permute-done((f32[64,128]{1,0:T(8,128)S(1)}, f32[64,128]{1,0:T(8,128)S(1)}, u32[]{:S(2)}, u32[]{:S(2)}) %collective-permute-start.62) | collective-permute-done | bytes 32800 | tf_op jit(solution)/shard_map/ppermute | solution.py:364
  63.3 0.0 copy-done
  63.3 0.0 copy-done.1
  63.3 0.7 %shard_map.133 = f32[3,32,128]{2,1,0:T(8,128)} custom-call(f32[3,64,128]{2,1,0:T(8,128)S(1)} %shard_map.132.total_ref, f32[64,128]{1,0:T(8,128)S(1)} %collective-permute-done.62.low_ref, f32[64,128]{1,0:T(8,128)S(1)} %collective-permute-done.63.high_ref, f32[3,32,128]{2,1,0:T(8,128)S(1)} %bitcast.20, f32[3,32,128]{2,1,0:T(8,128)S(1)} %bitcast.21), custom_call_target="tpu_custom_call" | custom-call | flops 100000 | bytes 300000 | tf_op jit(solution)/shard_map/pallas_call | solution.py:366
  (2 shorter events, 0.0 us)
Async XLA Ops:
  0.6 13.1 %copy-start.3 = (bf16[1,1,2,128,512]{4,3,2,1,0:T(8,128)(2,1)S(1)}, bf16[1,1,2,128,512]{4,3,2,1,0:T(8,128)(2,1)}, u32[]{:S(2)}) copy-start(bf16[1,1,2,128,512]{4,3,2,1,0:T(8,128)(2,1)} %param.77) | copy-start | bytes 786436
  3.3 10.4 %collective-permute-start.3 = (bf16[128,512]{1,0:T(8,128)(2,1)}, bf16[128,512]{1,0:T(8,128)(2,1)}, u32[]{:S(2)}, u32[]{:S(2)}) collective-permute-start(bf16[128,512]{1,0:T(8,128)(2,1)} %get-tuple-element.876), channel_id=1, source_target_pairs={{4,0},{5,1},{6,2},{7,3},{8,4},{9,5},{10,6},{11,7},{12,8},{13,9},{1... | collective-permute-start | bytes 393224 | tf_op jit(solution)/shard_map/cond/branch_4_fun/ppermute | solution.py:324
  13.7 12.4 %copy-start.2 = (f32[1,1,2,128,512]{4,3,2,1,0:T(8,128)S(1)}, f32[1,1,2,128,512]{4,3,2,1,0:T(8,128)}, u32[]{:S(2)}) copy-start(f32[1,1,2,128,512]{4,3,2,1,0:T(8,128)} %param.76) | copy-start | bytes 1572868
  13.7 12.2 %collective-permute-start.32 = (bf16[128,512]{1,0:T(8,128)(2,1)}, bf16[128,512]{1,0:T(8,128)(2,1)}, u32[]{:S(2)}, u32[]{:S(2)}) collective-permute-start(bf16[128,512]{1,0:T(8,128)(2,1)} %get-tuple-element.1202), channel_id=1, source_target_pairs={{2,0},{3,1},{4,2},{5,3},{6,4},{7,5},{8,6},{9,7},{10,8},{11,9},{12,... | collective-permute-start | bytes 393224 | tf_op jit(solution)/shard_map/cond/branch_2_fun/ppermute | solution.py:324
  30.1 33.2 %copy-start = (f32[1,1,3,4096]{3,1,2,0:T(1,128)S(1)}, f32[1,1,3,4096]{3,1,2,0:T(1,128)}, u32[]{:S(2)}) copy-start(f32[1,1,3,4096]{3,1,2,0:T(1,128)} %param.86) | copy-start | bytes 147460
  30.1 33.2 %copy-start.1 = (f32[1,1,3,4096]{3,1,2,0:T(1,128)S(1)}, f32[1,1,3,4096]{3,1,2,0:T(1,128)}, u32[]{:S(2)}) copy-start(f32[1,1,3,4096]{3,1,2,0:T(1,128)} %param.87) | copy-start | bytes 147460
  55.2 5.9 %collective-permute-start.63 = (f32[64,128]{1,0:T(8,128)S(1)}, f32[64,128]{1,0:T(8,128)S(1)}, u32[]{:S(2)}, u32[]{:S(2)}) collective-permute-start(f32[64,128]{1,0:T(8,128)S(1)} %get-tuple-element.1500), channel_id=1, source_target_pairs={{32,0},{64,32},{96,64},{128,96},{160,128},{192,160},{224,192},{256... | collective-permute-start | bytes 98312 | tf_op jit(solution)/shard_map/ppermute | solution.py:365
  57.5 5.8 %collective-permute-start.62 = (f32[64,128]{1,0:T(8,128)S(1)}, f32[64,128]{1,0:T(8,128)S(1)}, u32[]{:S(2)}, u32[]{:S(2)}) collective-permute-start(f32[64,128]{1,0:T(8,128)S(1)} %get-tuple-element.1501), channel_id=1, source_target_pairs={{0,32},{32,64},{64,96},{96,128},{128,160},{160,192},{192,224},{224... | collective-permute-start | bytes 98312 | tf_op jit(solution)/shard_map/ppermute | solution.py:364

commit v5 on v4

--- a/solution.py
+++ b/solution.py
@@ -163,10 +163,8 @@
             blocks_ref[r + 1] = jnp.where(left, there, here).astype(bf16)
 
 
-def stay_kernel(tile_hbm, out_hbm, sem):
-    copy = pltpu.make_async_copy(tile_hbm, out_hbm, sem)
-    copy.start()
-    copy.wait()
+def stay_kernel(tile_ref, out_ref):
+    out_ref[...] = tile_ref[...]
 
 
 def main_kernel(
@@ -232,27 +230,25 @@
         store.wait()
 
 
-def sum_kernel(arrived_ref, total_ref):
+def sum_kernel(arrived_ref, *total_refs):
     left = lax.broadcasted_iota(jnp.int32, (BS, LANE), 1) < BS
     sums = []
     for part in range(2):
         def body(j, acc):
-            head = arrived_ref[j, pl.ds(2 * BS, 8), :].astype(f32)[:1]
+            head = jnp.broadcast_to(arrived_ref[j, pl.ds(2 * BS, 8), :].astype(f32)[:1], (BS, LANE))
             value = arrived_ref[j, pl.ds(part * BS, BS), :].astype(f32)
-            return tuple(
-                acc[s] + jnp.where(jnp.broadcast_to(head == s, (BS, LANE)), value, 0.0) for s in range(PATCHES)
-            )
-
-        acc = lax.fori_loop(0, TILES, body, tuple(jnp.zeros((BS, LANE), f32) for _ in range(PATCHES)), unroll=4)
+            return tuple(acc[s] + jnp.where(head == s, value, 0.0) for s in range(PATCHES))
+
+        acc = lax.fori_loop(0, TILES, body, tuple(jnp.zeros((BS, LANE), f32) for _ in range(PATCHES)), unroll=8)
         sums.append([a + pltpu.roll(a, BS, 1) for a in acc])
     for s in range(PATCHES):
-        total_ref[s] = jnp.where(left, sums[0][s], sums[1][s])
-
-
-def final_kernel(total_ref, low_ref, high_ref, sum_ref, weight_ref, out_ref, merged_ref):
+        total_refs[s][...] = jnp.where(left, sums[0][s], sums[1][s])
+
+
+def final_kernel(first_ref, middle_ref, last_ref, low_ref, high_ref, sum_ref, weight_ref, out_ref, merged_ref):
     left = lax.broadcasted_iota(jnp.int32, (BS // 2, LANE), 1) < BS
     for s in range(PATCHES):
-        merged = total_ref[s]
+        merged = (first_ref, middle_ref, last_ref)[s][...]
         if s == 0:
             merged = merged + low_ref[...]
         if s == PATCHES - 1:
@@ -314,7 +310,7 @@
     )
 
     stay = call(
-        stay_kernel, sds((H, W), bf16), [ANY], (0, 300_000), [pltpu.SemaphoreType.DMA], ANY
+        stay_kernel, sds((H, W), bf16), [VMEM], (0, 300_000)
     )
 
     def shifted(d, beside):
@@ -357,20 +353,20 @@
     )(origin, first, second, band, both, weights, science[0, 0], inverse_variance[0, 0])
 
     total = call(
-        sum_kernel, sds((PATCHES, BS, LANE), f32), [VMEM], (5_000_000, 1_300_000)
+        sum_kernel, (sds((BS, LANE), f32),) * PATCHES, [VMEM], (5_000_000, 1_300_000)
     )(all_to_all(payload))
 
     count = lax.axis_size("sky")
-    low = lax.ppermute(total[PATCHES - 1], "sky", [(i, i + 1) for i in range(count - 1)])
+    low = lax.ppermute(total[-1], "sky", [(i, i + 1) for i in range(count - 1)])
     high = lax.ppermute(total[0], "sky", [(i + 1, i) for i in range(count - 1)])
     result = call(
         final_kernel,
         sds((PATCHES, BS // 2, LANE), f32),
-        [VMEM] * 5,
+        [VMEM] * 7,
         (100_000, 300_000),
         [pltpu.VMEM((BS, LANE), f32)],
     )(
-        total,
+        *total,
         low,
         high,
         coadd_sum[0, 0].reshape(PATCHES, BS // 2, LANE),

time: 64.7 us -> 65.3 us (level)
  the two profiles are of different devices: /device:TPU:64 before, /device:TPU:384 now
where the time goes in v5:
time: 65.3 us
  blocking collectives  22.6 us (35%)
  starting transfers between devices  15.5 us (24%)
  Pallas kernels  11.9 us (18%)
  waiting for transfers between devices  11.9 us (18%)
  between operations  2 us (3%)
  local copies, waits for them, and re-layouts  1.33 us (2%)
    all_to_all x1, blocking collectives, all_to_all(): return lax.all_to_all(x, 'tile', split_axis=0, concat_axis=0, tiled=True)  22.6 us
    ppermute x2, starting transfers between devices, branch(): lax.ppermute(tile, 'tile', pairs)  7.94 us
    pallas_call x2, Pallas kernels, branch(): beside(*args)  6.51 us
    ppermute x2, waiting for transfers between devices, branch(): lax.ppermute(tile, 'tile', pairs)  6.43 us
    ppermute x1, waiting for transfers between devices, shards(): low = lax.ppermute(total[-1], 'sky', [(i, i + 1) for i in range(count - 1)])  5.47 us
    ppermute x1, starting transfers between devices, shards(): high = lax.ppermute(total[0], 'sky', [(i + 1, i) for i in range(count - 1)])  5.4 us
    pallas_call x1, Pallas kernels, shards(): call(main_kernel, (sds((VISITS, H, W), f32), sds((TILES, 2 * BS + 8, LANE...  3.9 us
    ppermute x1, starting transfers between devices, shards(): low = lax.ppermute(total[-1], 'sky', [(i, i + 1) for i in range(count - 1)])  2.15 us
  transfers between devices with their start and end apart: 4, of which 3 were waited for; matrix products, arithmetic and copies ran while one was open for 0% of the time, Pallas kernels for 10%

profile of v5, /device:TPU:384, one launch (start us, length us, event | category | flops | bytes accessed | tf_op | source)
XLA Modules:
  0.0 65.3 jit_solution(5034873383524424132)
XLA Ops:
  0.6 0.0 copy-start.3
  0.6 1.3 %fusion = (s32[1,1]{1,0:T(1,128)}, s32[1,1]{1,0:T(1,128)}) fusion(s32[1,2]{1,0:T(1,128)} %param.82), kind=kLoop, calls=%fused_computation | loop fusion | bytes 16 | tf_op jit(solution)/shard_map/slice | solution.py:331
  3.3 9.6 %conditional.2 = (bf16[128,512]{1,0:T(8,128)(2,1)}, f32[64,128]{1,0:T(8,128)S(1)}, f32[128,256]{1,0:T(8,128)S(1)}, s32[64]{0:T(128)S(1)}, s32[64]{0:T(128)S(1)}) conditional(s32[]{:T(128)} %bitcast, (bf16[128,512]{1,0:T(8,128)(2,1)}, s32[32]{0:T(128)}, s32[32]{0:T(128)}, s32[2]{0:T(128)}, s32[2,20]{1,0:T(2,128)}, ...), branch_computations={%region_0.0_spmd, %region_1.0_spmd, %region_2.0_spmd, %region_3.0_... | conditional | flops 10000000 | bytes 1524368 | solution.py:327
  3.3 5.1 %collective-permute-start.16 = (bf16[128,512]{1,0:T(8,128)(2,1)}, bf16[128,512]{1,0:T(8,128)(2,1)}, u32[]{:S(2)}, u32[]{:S(2)}) collective-permute-start(bf16[128,512]{1,0:T(8,128)(2,1)} %get-tuple-element.1019), channel_id=1, source_target_pairs={{17,0},{18,1},{19,2},{20,3},{21,4},{22,5},{23,6},{24,7},{25,8},{26... | collective-permute-start | bytes 393224 | tf_op jit(solution)/shard_map/cond/branch_17_fun/ppermute | solution.py:320
  8.4 2.2 %branch_17_fun.2 = (f32[64,128]{1,0:T(8,128)S(1)}, f32[128,256]{1,0:T(8,128)S(1)}, s32[64]{0:T(128)S(1)}, s32[64]{0:T(128)S(1)}) custom-call(s32[32]{0:T(128)} %get-tuple-element.1020.owner_ref, s32[32]{0:T(128)} %get-tuple-element.1021.slot_ref, s32[2]{0:T(128)} %get-tuple-element.1022.count_ref, s32[2,20]{1,0:T(2,128)} %get-tuple-element.1023.index_ref, ...), custom_call_target="tpu_custom_call" | custom-call | flops 10000000 | bytes 1000000 | tf_op jit(solution)/shard_map/cond/branch_17_fun/pallas_call | solution.py:320
  10.6 2.2 %collective-permute-done.16 = bf16[128,512]{1,0:T(8,128)(2,1)} collective-permute-done((bf16[128,512]{1,0:T(8,128)(2,1)}, bf16[128,512]{1,0:T(8,128)(2,1)}, u32[]{:S(2)}, u32[]{:S(2)}) %collective-permute-start.16) | collective-permute-done | bytes 131104 | tf_op jit(solution)/shard_map/cond/branch_17_fun/ppermute | solution.py:320
  12.8 0.0 copy-done.3
  12.8 11.4 %conditional.3 = (bf16[128,512]{1,0:T(8,128)(2,1)}, bf16[1024,256]{1,0:T(8,128)(2,1)S(1)}, bf16[2,512,1024]{2,1,0:T(8,128)(2,1)S(1)}, bf16[32,72,128]{2,1,0:T(8,128)(2,1)S(1)}) conditional(s32[]{:T(128)} %bitcast.8, (bf16[128,512]{1,0:T(8,128)(2,1)}, s32[64]{0:T(128)S(1)}, s32[64]{0:T(128)S(1)}, ...), branch_computations={%region_32.0_spmd, %region_33.0_spmd, %region_34.0_spmd, %region_3... | conditional | flops 10000000 | bytes 3524360 | solution.py:330
  12.8 2.8 %collective-permute-start.59 = (bf16[128,512]{1,0:T(8,128)(2,1)}, bf16[128,512]{1,0:T(8,128)(2,1)}, u32[]{:S(2)}, u32[]{:S(2)}) collective-permute-start(bf16[128,512]{1,0:T(8,128)(2,1)} %get-tuple-element.1445), channel_id=1, source_target_pairs={{29,0},{30,1},{31,2},{0,3},{1,4},{2,5},{3,6},{4,7},{5,8},{6,9},{7,... | collective-permute-start | bytes 393224 | tf_op jit(solution)/shard_map/cond/branch_29_fun/ppermute | solution.py:320
  15.7 4.3 %branch_29_fun.3 = (bf16[1024,256]{1,0:T(8,128)(2,1)S(1)}, bf16[2,512,1024]{2,1,0:T(8,128)(2,1)S(1)}, bf16[32,72,128]{2,1,0:T(8,128)(2,1)S(1)}) custom-call(s32[64]{0:T(128)S(1)} %get-tuple-element.1446.from_ref, s32[64]{0:T(128)S(1)} %get-tuple-element.1447.slots_ref, f32[64,128]{1,0:T(8,128)S(1)} %get-tuple-element.1448.eff_ref, ...), custom_call_target="tpu_custom_call" | custom-call | flops 10000000 | bytes 3000000 | tf_op jit(solution)/shard_map/cond/branch_29_fun/pallas_call | solution.py:320
  20.0 4.2 %collective-permute-done.59 = bf16[128,512]{1,0:T(8,128)(2,1)} collective-permute-done((bf16[128,512]{1,0:T(8,128)(2,1)}, bf16[128,512]{1,0:T(8,128)(2,1)}, u32[]{:S(2)}, u32[]{:S(2)}) %collective-permute-start.59) | collective-permute-done | bytes 131104 | tf_op jit(solution)/shard_map/cond/branch_29_fun/ppermute | solution.py:320
  24.2 0.0 copy-done.2
  24.2 3.9 %shard_map.131 = (f32[2,128,512]{2,1,0:T(8,128)}, bf16[32,136,128]{2,1,0:T(8,128)(2,1)S(1)}) custom-call(s32[64]{0:T(128)S(1)} %get-tuple-element.1488.from_ref, bf16[128,512]{1,0:T(8,128)(2,1)} %get-tuple-element.1489.tile0_ref, bf16[128,512]{1,0:T(8,128)(2,1)} %get-tuple-element.1493.tile1_ref, bf16[1024,256]{1,0:T(8,128)(2,1)S(1)} %get-tuple-element.1494.band_ref, ...), custom_call_target="tpu_custom_call" | custom-call | flops 2000000000 | bytes 6000000 | tf_op jit(solution)/shard_map/pallas_call | solution.py:337
  28.1 0.0 copy-start
  28.2 0.0 copy-start.1
  28.2 22.6 %all_to_all.5.arrived_ref = bf16[32,136,128]{2,1,0:T(8,128)(2,1)S(1)} all-to-all(bf16[32,136,128]{2,1,0:T(8,128)(2,1)S(1)} %get-tuple-element.1498), channel_id=1, replica_groups=mesh['sky'=16,'tile'=32] {'tile'}, dimensions={0} | all-to-all | bytes 2228224 | tf_op jit(solution)/shard_map/all_to_all | solution.py:265
  50.8 0.7 %shard_map.132 = (f32[64,128]{1,0:T(8,128)S(1)}, f32[64,128]{1,0:T(8,128)S(1)}, f32[64,128]{1,0:T(8,128)S(1)}) custom-call(bf16[32,136,128]{2,1,0:T(8,128)(2,1)S(1)} %all_to_all.5.arrived_ref), custom_call_target="tpu_custom_call" | custom-call | flops 5000000 | bytes 1300000 | tf_op jit(solution)/shard_map/pallas_call | solution.py:355
  51.6 5.4 %collective-permute-start.63 = (f32[64,128]{1,0:T(8,128)S(1)}, f32[64,128]{1,0:T(8,128)S(1)}, u32[]{:S(2)}, u32[]{:S(2)}) collective-permute-start(f32[64,128]{1,0:T(8,128)S(1)} %get-tuple-element.1499.first_ref), channel_id=1, source_target_pairs={{32,0},{64,32},{96,64},{128,96},{160,128},{192,160},{224,192},{256... | collective-permute-start | bytes 98312 | tf_op jit(solution)/shard_map/ppermute | solution.py:361
  57.0 2.1 %collective-permute-start.62 = (f32[64,128]{1,0:T(8,128)S(1)}, f32[64,128]{1,0:T(8,128)S(1)}, u32[]{:S(2)}, u32[]{:S(2)}) collective-permute-start(f32[64,128]{1,0:T(8,128)S(1)} %get-tuple-element.1501.last_ref), channel_id=1, source_target_pairs={{0,32},{32,64},{64,96},{96,128},{128,160},{160,192},{192,224},{224... | collective-permute-start | bytes 98312 | tf_op jit(solution)/shard_map/ppermute | solution.py:360
  59.1 0.0 collective-permute-done.63.high_ref
  59.1 5.5 %collective-permute-done.62.low_ref = f32[64,128]{1,0:T(8,128)S(1)} collective-permute-done((f32[64,128]{1,0:T(8,128)S(1)}, f32[64,128]{1,0:T(8,128)S(1)}, u32[]{:S(2)}, u32[]{:S(2)}) %collective-permute-start.62) | collective-permute-done | bytes 32800 | tf_op jit(solution)/shard_map/ppermute | solution.py:360
  64.6 0.0 copy-done
  64.6 0.0 copy-done.1
  64.6 0.7 %shard_map.133 = f32[3,32,128]{2,1,0:T(8,128)} custom-call(f32[64,128]{1,0:T(8,128)S(1)} %get-tuple-element.1499.first_ref, f32[64,128]{1,0:T(8,128)S(1)} %get-tuple-element.1500.middle_ref, f32[64,128]{1,0:T(8,128)S(1)} %get-tuple-element.1501.last_ref, f32[64,128]{1,0:T(8,128)S(1)} %collective-permute-done.62.low_ref, ...), custom_call_target="tpu_custom_call" | custom-call | flops 100000 | bytes 300000 | tf_op jit(solution)/shard_map/pallas_call | solution.py:362
  (1 shorter events, 0.0 us)
Async XLA Ops:
  0.6 12.2 %copy-start.3 = (bf16[1,1,2,128,512]{4,3,2,1,0:T(8,128)(2,1)S(1)}, bf16[1,1,2,128,512]{4,3,2,1,0:T(8,128)(2,1)}, u32[]{:S(2)}) copy-start(bf16[1,1,2,128,512]{4,3,2,1,0:T(8,128)(2,1)} %param.77) | copy-start | bytes 786436
  3.3 9.5 %collective-permute-start.16 = (bf16[128,512]{1,0:T(8,128)(2,1)}, bf16[128,512]{1,0:T(8,128)(2,1)}, u32[]{:S(2)}, u32[]{:S(2)}) collective-permute-start(bf16[128,512]{1,0:T(8,128)(2,1)} %get-tuple-element.1019), channel_id=1, source_target_pairs={{17,0},{18,1},{19,2},{20,3},{21,4},{22,5},{23,6},{24,7},{25,8},{26... | collective-permute-start | bytes 393224 | tf_op jit(solution)/shard_map/cond/branch_17_fun/ppermute | solution.py:320
  12.8 11.4 %copy-start.2 = (f32[1,1,2,128,512]{4,3,2,1,0:T(8,128)S(1)}, f32[1,1,2,128,512]{4,3,2,1,0:T(8,128)}, u32[]{:S(2)}) copy-start(f32[1,1,2,128,512]{4,3,2,1,0:T(8,128)} %param.76) | copy-start | bytes 1572868
  12.8 11.4 %collective-permute-start.59 = (bf16[128,512]{1,0:T(8,128)(2,1)}, bf16[128,512]{1,0:T(8,128)(2,1)}, u32[]{:S(2)}, u32[]{:S(2)}) collective-permute-start(bf16[128,512]{1,0:T(8,128)(2,1)} %get-tuple-element.1445), channel_id=1, source_target_pairs={{29,0},{30,1},{31,2},{0,3},{1,4},{2,5},{3,6},{4,7},{5,8},{6,9},{7,... | collective-permute-start | bytes 393224 | tf_op jit(solution)/shard_map/cond/branch_29_fun/ppermute | solution.py:320
  28.1 36.5 %copy-start = (f32[1,1,3,4096]{3,1,2,0:T(1,128)S(1)}, f32[1,1,3,4096]{3,1,2,0:T(1,128)}, u32[]{:S(2)}) copy-start(f32[1,1,3,4096]{3,1,2,0:T(1,128)} %param.86) | copy-start | bytes 147460
  28.2 36.4 %copy-start.1 = (f32[1,1,3,4096]{3,1,2,0:T(1,128)S(1)}, f32[1,1,3,4096]{3,1,2,0:T(1,128)}, u32[]{:S(2)}) copy-start(f32[1,1,3,4096]{3,1,2,0:T(1,128)} %param.87) | copy-start | bytes 147460
  51.6 7.6 %collective-permute-start.63 = (f32[64,128]{1,0:T(8,128)S(1)}, f32[64,128]{1,0:T(8,128)S(1)}, u32[]{:S(2)}, u32[]{:S(2)}) collective-permute-start(f32[64,128]{1,0:T(8,128)S(1)} %get-tuple-element.1499.first_ref), channel_id=1, source_target_pairs={{32,0},{64,32},{96,64},{128,96},{160,128},{192,160},{224,192},{256... | collective-permute-start | bytes 98312 | tf_op jit(solution)/shard_map/ppermute | solution.py:361
  57.0 7.6 %collective-permute-start.62 = (f32[64,128]{1,0:T(8,128)S(1)}, f32[64,128]{1,0:T(8,128)S(1)}, u32[]{:S(2)}, u32[]{:S(2)}) collective-permute-start(f32[64,128]{1,0:T(8,128)S(1)} %get-tuple-element.1501.last_ref), channel_id=1, source_target_pairs={{0,32},{32,64},{64,96},{96,128},{128,160},{160,192},{192,224},{224... | collective-permute-start | bytes 98312 | tf_op jit(solution)/shard_map/ppermute | solution.py:360
